TPU v7x, 128 devices: a whole 4x4x4 slice. The times are simulated.
128 devices in a mesh: prow: 8 (over x, z_lo), pcol: 16 (over z_hi, y, core).
Axes of the slice: x: 4, y: 4, z: 4 (z_hi: 2, z_lo: 2; z = z_hi * 2 + z_lo), core: 2. Of those that a mesh axis runs over, the one named last changes fastest.
Arguments:
- ancestor_inverse: float32 [4096, 4096], P('prow', 'pcol'), may hold values from -6 to 6
- lower_panel: float32 [4096, 2, 2048], P('prow'), may hold values from -0.09375 to 0.09375
- pivot_inverse: float32 [2, 2048, 2048], P(None, 'pcol', 'prow'), may hold values from -6 to 6
- structure: int32 [2, 64], replicated, may hold values from 0 to 1, as said below
Outputs:
- column_blocks: float32 [4096, 2, 2048], P(('prow', 'pcol'))
- diagonal_blocks: float32 [2, 2048, 2048], P(None, 'pcol', 'prow')
Inputs may be any that keep to these rules, and one draw needn't show every extreme that they name: structure[k, b] is 1 when ancestor rows 64 * b to 64 * b + 63 belong to supernode k's structure, else 0; the last block belongs to every supernode.
All inputs are finite; a program needn't handle non-finite values.
Results may differ from a plain program's by a relative error of at most 0.000082.
Values sent between devices are 32-bit elements; how exact they have to be, the bound alone decides.
A program may use at most 128 MiB of HBM per device.

v0:
```python
import jax
import jax.numpy as jnp
from jax import lax
from jax.sharding import PartitionSpec as P

S = 2048
NSUP = 2
BLK = 64


def spread(block, axis, holder):
    block = jnp.where(lax.axis_index(axis) == holder, block, jnp.zeros_like(block))
    return lax.psum(block, axis)


def body(ancestor_inverse, lower_panel, pivot_inverse, structure):
    n_rows = lax.axis_size("prow")
    n_cols = lax.axis_size("pcol")
    row_index = lax.axis_index("prow")
    col_index = lax.axis_index("pcol")
    part_rows, part_cols = ancestor_inverse.shape
    ratio = n_cols // n_rows
    rows_dev = part_rows // n_cols
    col_width = S // n_cols
    nblocks = structure.shape[1]
    global_rows = row_index * part_rows + jnp.arange(part_rows, dtype=jnp.int32)
    onehot = (global_rows[:, None] // BLK == jnp.arange(nblocks, dtype=jnp.int32)[None, :]).astype(
        jnp.float32
    )
    row_mask = jnp.dot(onehot, structure.astype(jnp.float32).T, precision=lax.Precision.HIGHEST)
    masked = lower_panel * row_mask[:, :, None]

    def solve_group(masked_group, mask_group, pivot_group):
        width = masked_group.shape[1]
        offset = col_index % ratio * part_cols
        own_rows = lax.dynamic_slice_in_dim(masked_group, offset, part_cols, 0)
        panel = spread(own_rows, "prow", col_index // ratio)
        flat_panel = panel.reshape(part_cols, width * S)
        col_slice = lax.dynamic_slice_in_dim(masked_group, col_index * col_width, col_width, 2)
        result = jnp.dot(
            ancestor_inverse,
            flat_panel,
            precision=lax.Precision.HIGHEST,
            preferred_element_type=jnp.float32,
        )
        summed = lax.psum_scatter(
            result.reshape(lax.axis_size("pcol") * rows_dev, width, S),
            "pcol",
            scatter_dimension=0,
            tiled=True,
        )
        own_mask = lax.dynamic_slice_in_dim(mask_group, col_index * rows_dev, rows_dev, 0)
        solved = -own_mask[:, :, None] * summed
        partial_value = jnp.einsum(
            "aks,akt->kst",
            col_slice,
            lax.all_gather(solved, "pcol", axis=0, tiled=True),
            precision=lax.Precision.HIGHEST,
            preferred_element_type=jnp.float32,
        )
        sums = lax.psum_scatter(partial_value, "prow", scatter_dimension=2, tiled=True)
        return (solved, pivot_group - sums)

    results = [
        solve_group(
            masked[:, index : index + 1],
            row_mask[:, index : index + 1],
            pivot_inverse[index : index + 1],
        )
        for index in range(NSUP)
    ]
    column_blocks = jnp.concatenate([item[0] for item in results], axis=1)
    diagonal_blocks = jnp.concatenate([item[1] for item in results], axis=0)
    return (column_blocks, diagonal_blocks)


def solution(mesh):
    return jax.shard_map(
        body,
        mesh=mesh,
        in_specs=(P("prow", "pcol"), P("prow", None, None), P(None, "pcol", "prow"), P()),
        out_specs=(P(("prow", "pcol"), None, None), P(None, "pcol", "prow")),
        check_vma=False,
    )
```

profile of v0, /device:TPU:1, one launch (start us, length us, event | category | flops | bytes accessed | tf_op | source)
XLA Modules:
  0.0 618.3 jit_solution(10843036921663056735)
XLA Ops:
  7.3 1.0 fusion.16
  8.3 8.6 %copy_multiply_fusion = f32[512,2,2048]{2,0,1:T(8,128)S(1)} fusion(f32[512,2,2048]{2,1,0:T(2,128)} %param.5, f32[512,2]{0,1:T(2,128)S(1)} %fusion.16), kind=kLoop, calls=%fused_computation | loop fusion | flops 2097152 | bytes 16781312 | tf_op jit(solution)/shard_map/mul | solution.py:31
  16.9 3.8 fusion.28
  20.7 4.9 select_bitcast_fusion
  25.6 0.2 all-reduce.7.cloned.1.call-start
  25.8 184.9 %all-reduce.9.cloned.1.call-done = (f32[256,2048]{1,0:T(8,128)}, f32[256,2048]{1,0:T(8,128)}) async-done(((f32[256,2048]{1,0:T(8,128)}, f32[256,2048]{1,0:T(8,128)}), (f32[256,2048]{1,0:T(8,128)}, f32[256,2048]{1,0:T(8,128)})) %all-reduce.9.cloned.1.call-update) | async-done | bytes 4194320 | tf_op jit(solution)/shard_map/psum | solution.py:13
  210.7 9.8 %convolution_bitcast_fusion = f32[512,1,2048]{0,2,1:T(8,128)} fusion(f32[256,2048]{1,0:T(8,128)} %get-tuple-element.10, f32[512,256]{1,0:T(8,128)S(1)} %copy-done), kind=kOutput, calls=%fused_computation.7 | convolution fusion | flops 3221225472 | bytes 6815744 | tf_op jit(solution)/shard_map/dot_general | solution.py:40
  220.5 11.1 %copy.12 = f32[512,1,2048]{2,1,0:T(1,128)} copy(f32[512,1,2048]{0,2,1:T(8,128)} %convolution_bitcast_fusion) | data formatting | bytes 8388608 | tf_op jit(solution)/shard_map/reshape | solution.py:47
  231.7 8.2 %convolution_bitcast_fusion.1 = f32[512,1,2048]{0,2,1:T(8,128)} fusion(f32[256,2048]{1,0:T(8,128)S(1)} %copy-done.3, f32[512,256]{1,0:T(8,128)S(1)} %copy-done), kind=kOutput, calls=%fused_computation.8 | convolution fusion | flops 3221225472 | bytes 6815744 | tf_op jit(solution)/shard_map/dot_general | solution.py:40
  239.8 11.0 %copy.11 = f32[512,1,2048]{2,1,0:T(1,128)} copy(f32[512,1,2048]{0,2,1:T(8,128)} %convolution_bitcast_fusion.1) | data formatting | bytes 8388608 | tf_op jit(solution)/shard_map/reshape | solution.py:47
  250.9 0.0 all-gather.3.cloned.1.call-start
  251.0 0.6 copy-done.5
  251.5 0.6 dynamic-slice
  252.8 0.1 fusion.25
  252.9 161.8 %all-reduce.7.cloned.1.call-done = (f32[512,1,2048]{2,1,0:T(1,128)}, f32[512,1,2048]{2,1,0:T(1,128)}) async-done(((f32[512,1,2048]{2,1,0:T(1,128)}, f32[512,1,2048]{2,1,0:T(1,128)}), (f32[512,1,2048]{2,1,0:T(1,128)}, f32[512,1,2048]{2,1,0:T(1,128)})) %all-reduce.7.cloned.1.call-update) | async-done | bytes 8388624
  414.7 1.9 dynamic-slice_multiply_fusion.1
  416.6 0.0 all-gather.5.cloned.1.call-start
  416.7 0.1 fusion.27
  416.7 1.9 dynamic-slice_multiply_fusion
  418.7 0.0 reduce-scatter.3.cloned.1.call-start
  418.7 57.3 %all-gather.3.cloned.1.call-done = f32[512,1,2048]{2,1,0:T(1,128)} async-done(((f32[32,1,2048]{2,1,0:T(1,128)}), f32[512,1,2048]{2,1,0:T(1,128)}) %all-gather.3.cloned.1.call-update) | async-done | bytes 4194320 | tf_op jit(solution)/shard_map/all_gather | solution.py:57
  476.0 6.8 %fusion.6 = f32[1,128,2048]{2,1,0:T(8,128)} fusion(f32[512,1,2048]{2,1,0:T(1,128)} %all-gather.3.cloned.1.call-done, f32[512,1,2048]{2,0,1:T(8,128)} %get-tuple-element.12, s32[]{:T(128)S(6)} %select_n.56), kind=kOutput, calls=%fused_computation.9 | convolution fusion | flops 1610612736 | bytes 5505028 | tf_op jit(solution)/shard_map/aks,akt->kst/dot_general | solution.py:54
  482.8 0.3 reduce-scatter.5.cloned.1.call-start
  483.0 50.6 %all-gather.5.cloned.1.call-done = f32[512,1,2048]{2,1,0:T(1,128)} async-done(((f32[32,1,2048]{2,1,0:T(1,128)}), f32[512,1,2048]{2,1,0:T(1,128)}) %all-gather.5.cloned.1.call-update) | async-done | bytes 4194320 | tf_op jit(solution)/shard_map/all_gather | solution.py:57
  533.7 6.7 %fusion.9 = f32[1,128,2048]{2,1,0:T(8,128)} fusion(f32[512,1,2048]{2,1,0:T(1,128)} %all-gather.5.cloned.1.call-done, f32[512,1,2048]{2,0,1:T(8,128)} %get-tuple-element.13, s32[]{:T(128)S(6)} %select_n.56), kind=kOutput, calls=%fused_computation.10 | convolution fusion | flops 1610612736 | bytes 5505028 | tf_op jit(solution)/shard_map/aks,akt->kst/dot_general | solution.py:54
  540.5 0.1 copy.13
  540.6 0.1 copy.14
  540.7 1.2 copy.15
  541.9 26.8 %reduce-scatter.3.cloned.1.call-done = f32[1,128,256]{2,1,0:T(8,128)} async-done(((f32[1,128,2048]{2,1,0:T(8,128)}), f32[1,128,256]{2,1,0:T(8,128)}) %reduce-scatter.3.cloned.1.call-update) | async-done | bytes 131088 | tf_op jit(solution)/shard_map/reduce_scatter | solution.py:61
  568.7 41.1 %reduce-scatter.5.cloned.1.call-done = f32[1,128,256]{2,1,0:T(8,128)} async-done(((f32[1,128,2048]{2,1,0:T(8,128)}), f32[1,128,256]{2,1,0:T(8,128)}) %reduce-scatter.5.cloned.1.call-update) | async-done | bytes 131088 | tf_op jit(solution)/shard_map/reduce_scatter | solution.py:61
  609.7 1.0 slice_subtract_fusion.1
  610.7 0.7 pad_maximum_fusion.1
  (21 shorter events, 0.2 us)
Async XLA Ops:
  7.2 203.5 %copy-start = (f32[512,256]{1,0:T(8,128)S(1)}, f32[512,256]{1,0:T(8,128)}, u32[]{:S(2)}) copy-start(f32[512,256]{1,0:T(8,128)} %param.4) | copy-start | bytes 1572868
  7.2 203.5 %all-reduce.9.cloned.1.call-start = ((), (), s32[]{:S(2)}) async-start(), calls=%async_computation.7 | async-start | bytes 8388608 | tf_op jit(solution)/shard_map/psum | solution.py:13
  25.6 389.1 %all-reduce.7.cloned.1.call-start = ((), (), s32[]{:S(2)}) async-start(), calls=%async_computation.6 | async-start | bytes 16777216
  220.5 11.1 %copy-start.3 = (f32[256,2048]{1,0:T(8,128)S(1)}, f32[256,2048]{1,0:T(8,128)}, u32[]{:S(2)}) copy-start(f32[256,2048]{1,0:T(8,128)} %get-tuple-element.11) | copy-start | bytes 6291460
  250.9 0.7 copy-start.5
  250.9 225.1 %all-gather.3.cloned.1.call-start = ((), (), s32[]{:S(2)}) async-start(), calls=%async_computation.2 | async-start | bytes 4456448 | tf_op jit(solution)/shard_map/all_gather | solution.py:57
  416.6 117.1 %all-gather.5.cloned.1.call-start = ((), (), s32[]{:S(2)}) async-start(), calls=%async_computation.4 | async-start | bytes 4456448 | tf_op jit(solution)/shard_map/all_gather | solution.py:57
  418.7 150.0 %reduce-scatter.3.cloned.1.call-start = ((), (), s32[]{:S(2)}) async-start(), calls=%async_computation.3 | async-start | bytes 1179648 | tf_op jit(solution)/shard_map/reduce_scatter | solution.py:61
  482.7 57.7 %copy-start.1 = (f32[32,1,2048]{2,1,0:T(1,128)S(1)}, f32[32,1,2048]{2,1,0:T(1,128)}, u32[]{:S(2)}) copy-start(f32[32,1,2048]{2,1,0:T(1,128)} %dynamic-slice_multiply_fusion.1) | copy-start | bytes 786436
  482.7 57.8 %copy-start.2 = (f32[32,1,2048]{2,1,0:T(1,128)S(1)}, f32[32,1,2048]{2,1,0:T(1,128)}, u32[]{:S(2)}) copy-start(f32[32,1,2048]{2,1,0:T(1,128)} %dynamic-slice_multiply_fusion) | copy-start | bytes 786436
  482.8 127.0 %copy-start.4 = (f32[2,128,256]{2,1,0:T(8,128)S(1)}, f32[2,128,256]{2,1,0:T(8,128)}, u32[]{:S(2)}) copy-start(f32[2,128,256]{2,1,0:T(8,128)} %param.6) | copy-start | bytes 786436
  482.8 127.0 %reduce-scatter.5.cloned.1.call-start = ((), (), s32[]{:S(2)}) async-start(), calls=%async_computation.5 | async-start | bytes 1179648 | tf_op jit(solution)/shard_map/reduce_scatter | solution.py:61
Sparse Core Ops, SparseCore 0:
  25.7 184.9 all-reduce.8
  251.0 163.6 all-reduce.6
  417.7 58.2 all-gather.2
  478.8 54.7 all-gather.4
  535.9 32.6 reduce-scatter.2
  570.9 38.7 reduce-scatter.4
where the time goes:
time: 624 us; the launch traced here: 618 us
  waiting for transfers between devices  523 us (84%)
  matrix products  32.6 us (5%)
  local copies, waits for them, and re-layouts  28.5 us (5%)
  other arithmetic  19.1 us (3%)
  between operations  14.9 us (2%)
    psum x1, waiting for transfers between devices, spread(): return lax.psum(block, axis)  185 us
    unnamed x7, waiting for transfers between devices  162 us
    all_gather x2, waiting for transfers between devices, solve_group(): lax.all_gather(solved, 'pcol', axis=0, tiled=True)  108 us
    reduce_scatter x2, waiting for transfers between devices, solve_group(): lax.psum_scatter(partial_value, 'prow', scatter_dimension=2, tiled=True)  67.8 us
    reshape x2, local copies, waits for them, and re-layouts, solve_group(): result.reshape(lax.axis_size('pcol') * rows_dev, width, S)  22.1 us
    dot_general x2, matrix products, solve_group(): jnp.dot(ancestor_inverse, flat_panel, precision=lax.Precision.HIGHEST, pr...  18 us
    dot_general x2, matrix products, solve_group(): jnp.einsum('aks,akt->kst', col_slice, lax.all_gather(solved, 'pcol', axis...  13.5 us
  transfers between devices with their start and end apart: 6, of which 6 were waited for; matrix products, arithmetic and copies ran while one was open for 3% of the time, Pallas kernels for 0%

commit v1 on v0

v1 whole, which is shorter than its diff:
```python
import functools

import jax
import jax.numpy as jnp
from jax import lax
from jax.experimental import pallas as pl
from jax.experimental.pallas import tpu as pltpu
from jax.sharding import PartitionSpec as P

MESH = pl.DeviceIdType.MESH
F32 = jnp.float32
BF16 = jnp.bfloat16
S = 2048
NSUP = 2
BLK = 64
NX, NY, NZ = 4, 4, 4
NR, NC = 8, 16
W = 512
NCH = NSUP * S // W
PER_K = S // W
T = S // NC


def split(v):
    hi = v.astype(BF16)
    return hi, (v - hi.astype(F32)).astype(BF16)


def dot3(ahi, alo, bhi, blo):
    dot = functools.partial(jnp.dot, preferred_element_type=F32)
    return dot(ahi, bhi) + (dot(ahi, blo) + dot(alo, bhi))


def kernel(
    a_hbm, l_hbm, piv, structure, out_c, out_d,
    lst, xhi, xlo, abuf, ahi, alo, ybuf, zr, xo, xf, cbuf, dbuf, dxo, dxf, dsum, dfin,
    l_sem, a_send, a_recv, z_send, z_recv, xo_send, xo_recv, xf_send, xf_recv,
    c_send, c_recv, dxo_send, dxo_recv, dxf_send, dxf_recv, d_send, d_recv,
):
    pr, pc = lax.axis_index("prow"), lax.axis_index("pcol")
    rem, div = lax.rem, lax.div
    x, zl = div(pr, 2), rem(pr, 2)
    zh, rest = div(pc, 8), rem(pc, 8)
    z = 2 * zh + zl
    home, side = div(pc, 2), rem(pc, 2)

    def at_z(zz):
        return (x * 2 + rem(zz, 2), div(zz, 2) * 8 + rest)

    def at_x(xx):
        return (xx * 2 + zl, pc)

    z_down, z_up = at_z(rem(z + 3, 4)), at_z(rem(z + 1, 4))
    x_next, x_prev, x_far = rem(x + 1, 4), rem(x + 3, 4), rem(x + 2, 4)
    right, left = at_x(x_next), at_x(x_prev)
    is_home = home == pr

    def remote(src, dst, send, recv, device):
        return pltpu.make_async_remote_copy(
            src_ref=src, dst_ref=dst, send_sem=send, recv_sem=recv,
            device_id=device, device_id_type=MESH,
        )

    def await_bytes(ref, sem):
        pltpu.make_async_copy(ref, ref, sem).wait()

    rows = S * NSUP * BLK // 128
    l_copies = [
        pltpu.make_async_copy(
            l_hbm.at[pl.ds(i * rows, rows)], lst.at[pl.ds(i * rows, rows)], l_sem.at[i]
        )
        for i in range(NR)
    ]
    for copy in l_copies:
        copy.start()

    barrier = pltpu.get_barrier_semaphore()

    def greet(device):
        pl.semaphore_signal(barrier, inc=1, device_id=device, device_id_type=MESH)

    for device in (z_down, z_up, right, left):
        greet(device)
    for j in range(1, NC):
        greet((pr, rem(pc + j, NC)))
    for e in range(2):
        for j in range(1, NR):
            greet((rem(pr + j, NR), 2 * pr + e))

        @pl.when(2 * pr + e != pc)
        def _():
            greet((pr, 2 * pr + e))

    pl.semaphore_wait(barrier, jnp.where(is_home, 34, 35))

    home_zl = rem(home, 2)
    same = home_zl == zl

    def send_a(j):
        q = rem(pc + j, NC)
        z0 = 2 * div(q, 8) + zl
        for h in range(2):
            zt = rem(z0 + (1 if h == 0 else 3), 4)
            qt = jnp.where(same, q, div(zt, 2) * 8 + rem(q, 8))
            row = jnp.where(same, 128 + x * 32 + h * 16, h * 64 + x * 16)
            src = a_hbm.at[pl.ds(pl.multiple_of(q * 32 + h * 16, 16), 16)]
            dst = abuf.at[pl.ds(pl.multiple_of(row, 16), 16), pl.ds(pl.multiple_of(side * 256, 256), 256)]
            yield src, dst, (home, qt)

    for src, dst, device in send_a(0):
        @pl.when(is_home)
        def _():
            pltpu.make_async_copy(src, dst, a_recv).start()

        @pl.when(jnp.logical_not(is_home))
        def _():
            remote(src, dst, a_send, a_recv, device).start()

    @pl.loop(1, NC)
    def _(j):
        for src, dst, device in send_a(j):
            remote(src, dst, a_send, a_recv, device).start()

    @pl.loop(0, NR)
    def _(i):
        start = i * rows
        pltpu.make_async_copy(
            l_hbm.at[pl.ds(start, rows)], lst.at[pl.ds(start, rows)], l_sem.at[i]
        ).wait()
        for k in range(NSUP):
            mask = structure[k, pr * NR + i].astype(F32)
            for col in range(S // 128):
                v = lst[pl.ds(start + col * NSUP + k, BLK, stride=S * NSUP // 128), :] * mask
                hi, lo = split(v)
                xhi[k, pl.ds(i * BLK, BLK), pl.ds(col * 128, 128)] = hi
                xlo[k, pl.ds(i * BLK, BLK), pl.ds(col * 128, 128)] = lo

    await_bytes(abuf, a_recv)
    hi, lo = split(abuf[...])
    ahi[...] = hi
    alo[...] = lo

    def z_copies(j):
        cols = pl.ds(pl.multiple_of(j * W, W), W)
        return [
            remote(ybuf.at[pl.ds(h * 64, 64), cols], zr.at[h, :, cols], z_send, z_recv.at[h, j], device)
            for h, device in enumerate((z_down, z_up))
        ]

    @pl.loop(0, NCH)
    def _(j):
        cols = pl.ds(pl.multiple_of(j * W, W), W)
        k = div(j, PER_K)
        kcols = pl.ds(pl.multiple_of(rem(j, PER_K) * W, W), W)
        ybuf[:, cols] = dot3(ahi[...], alo[...], xhi[k, :, kcols], xlo[k, :, kcols])
        for copy in z_copies(j):
            copy.start()

    def x_stage(buf, row0, far, final, far_send, far_recv, final_send, final_recv):
        def first(j):
            cols = pl.ds(pl.multiple_of(j * W, W), W)
            return [
                remote(
                    buf.at[pl.ds(pl.multiple_of(row0 + x_far * 32 + h * 16, 16), 16), cols],
                    far.at[h, :, cols], far_send, far_recv.at[h, j], device,
                )
                for h, device in enumerate((right, left))
            ]

        def second(j):
            cols = pl.ds(pl.multiple_of(j * W, W), W)
            return [
                remote(
                    buf.at[pl.ds(pl.multiple_of(row0 + target * 32, 32), 32), cols],
                    final.at[h, :, cols], final_send, final_recv.at[h, j], device,
                )
                for h, (device, target) in enumerate(((right, x_next), (left, x_prev)))
            ]

        def send_first(j):
            for copy in first(j):
                copy.start()

        def send_second(j):
            cols = pl.ds(pl.multiple_of(j * W, W), W)
            for h, (copy, target) in enumerate(zip(first(j), (x_next, x_prev))):
                copy.wait_recv()
                rows_h = pl.ds(pl.multiple_of(row0 + target * 32 + h * 16, 16), 16)
                buf[rows_h, cols] += far[h, :, cols]
            for copy in second(j):
                copy.start()

        def total(j):
            cols = pl.ds(pl.multiple_of(j * W, W), W)
            for copy in second(j):
                copy.wait_recv()
            mine = pl.ds(pl.multiple_of(row0 + x * 32, 32), 32)
            return buf[mine, cols] + (final[0, :, cols] + final[1, :, cols])

        return send_first, send_second, total

    y_first, y_second, y_total = x_stage(ybuf, 128, xo, xf, xo_send, xo_recv, xf_send, xf_recv)
    d_first, d_second, d_total = x_stage(dbuf, 0, dxo, dxf, dxo_send, dxo_recv, dxf_send, dxf_recv)

    def add_z(j):
        cols = pl.ds(pl.multiple_of(j * W, W), W)
        for h, copy in enumerate(z_copies(j)):
            copy.wait_recv()
            for target in range(NX):
                ybuf[pl.ds(128 + target * 32 + h * 16, 16), cols] += zr[h, pl.ds(target * 16, 16), cols]
        y_first(j)

    def finish_c(j):
        cols = pl.ds(pl.multiple_of(j * W, W), W)
        k = div(j, PER_K)
        mask = structure[k, pr * NR + home].astype(F32)
        out_c[:, cols] = -mask * y_total(j)
        for i in range(W // T):
            q = rem(j, PER_K) * (W // T) + i
            src = out_c.at[:, pl.ds(pl.multiple_of(j * W + i * T, T), T)]
            dst = cbuf.at[k, pl.ds(pl.multiple_of(pc * 32, 32), 32)]

            @pl.when(q == pc)
            def _():
                pltpu.make_async_copy(src, dst, c_recv.at[k]).start()

            @pl.when(q != pc)
            def _():
                remote(src, dst, c_send, c_recv.at[k], (pr, q)).start()

    def second_product(k):
        await_bytes(cbuf.at[k], c_recv.at[k])
        chi, clo = split(cbuf[k].T)

        @pl.loop(0, PER_K)
        def _(n):
            j = k * PER_K + n
            cols = pl.ds(pl.multiple_of(j * W, W), W)
            kcols = pl.ds(pl.multiple_of(n * W, W), W)
            dbuf[:, cols] = dot3(chi, clo, xhi[k, :, kcols], xlo[k, :, kcols])
            d_first(j)

    def finish_d(j):
        cols = pl.ds(pl.multiple_of(j * W, W), W)
        k = div(j, PER_K)
        dsum[:, cols] = d_total(j)
        for i in range(W // T):
            q = rem(j, PER_K) * (W // T) + i
            src = dsum.at[:, pl.ds(pl.multiple_of(j * W + i * T, T), T)]
            dst = dfin.at[k, zl, pl.ds(pl.multiple_of(side * 128 + x * 32, 32), 32)]
            own = jnp.logical_and(is_home, q == pc)

            @pl.when(own)
            def _():
                pltpu.make_async_copy(src, dst, d_recv.at[k]).start()

            @pl.when(jnp.logical_not(own))
            def _():
                remote(src, dst, d_send, d_recv.at[k], (home, q)).start()

    @pl.loop(0, NCH)
    def _(j):
        add_z(j)

        @pl.when(j >= 1)
        def _():
            y_second(j - 1)

        @pl.when(j >= 2)
        def _():
            finish_c(j - 2)

    y_second(NCH - 1)
    second_product(0)
    finish_c(NCH - 2)
    finish_c(NCH - 1)

    @pl.loop(0, PER_K)
    def _(j):
        d_second(j)

    second_product(1)

    @pl.loop(0, PER_K)
    def _(j):
        finish_d(j)

    @pl.loop(PER_K, NCH)
    def _(j):
        d_second(j)

    @pl.loop(PER_K, NCH)
    def _(j):
        finish_d(j)

    for k in range(NSUP):
        await_bytes(dfin.at[k], d_recv.at[k])
        out_d[k] = piv[k] - (dfin[k, 0] + dfin[k, 1]).T

    await_bytes(abuf.at[pl.ds(0, 240)], a_send)

    @pl.when(jnp.logical_not(is_home))
    def _():
        await_bytes(abuf.at[pl.ds(0, 16)], a_send)

    await_bytes(zr, z_send)
    await_bytes(xo, xo_send)
    await_bytes(xf, xf_send)
    await_bytes(dxo, dxo_send)
    await_bytes(dxf, dxf_send)
    await_bytes(cbuf.at[:, pl.ds(0, 480)], c_send)
    await_bytes(dfin.at[:, :, pl.ds(0, 240)], d_send)

    @pl.when(jnp.logical_not(is_home))
    def _():
        await_bytes(dfin.at[:, :, pl.ds(0, 16)], d_send)


def body(ancestor_inverse, lower_panel, pivot_inverse, structure):
    part = lower_panel.shape[0]
    panel = lower_panel.reshape(part, NSUP, S // 128, 128).transpose(0, 2, 1, 3)
    panel = panel.reshape(part * NSUP * S // 128, 128)
    width = NSUP * S
    vmem = pl.BlockSpec(memory_space=pltpu.VMEM)
    hbm = pl.BlockSpec(memory_space=pl.ANY)
    dma = pltpu.SemaphoreType.DMA
    columns, diagonal = pl.pallas_call(
        kernel,
        name="selinv",
        out_shape=(
            jax.ShapeDtypeStruct((32, width), F32),
            jax.ShapeDtypeStruct(pivot_inverse.shape, F32),
        ),
        in_specs=[hbm, hbm, vmem, pl.BlockSpec(memory_space=pltpu.SMEM)],
        out_specs=(vmem, vmem),
        scratch_shapes=[
            pltpu.VMEM(panel.shape, F32),
            pltpu.VMEM((NSUP, part, S), BF16),
            pltpu.VMEM((NSUP, part, S), BF16),
            pltpu.VMEM((256, part), F32),
            pltpu.VMEM((256, part), BF16),
            pltpu.VMEM((256, part), BF16),
            pltpu.VMEM((256, width), F32),
            pltpu.VMEM((2, 64, width), F32),
            pltpu.VMEM((2, 16, width), F32),
            pltpu.VMEM((2, 32, width), F32),
            pltpu.VMEM((NSUP, part, T), F32),
            pltpu.VMEM((128, width), F32),
            pltpu.VMEM((2, 16, width), F32),
            pltpu.VMEM((2, 32, width), F32),
            pltpu.VMEM((32, width), F32),
            pltpu.VMEM((NSUP, 2, 256, 128), F32),
            dma((NR,)),
            dma(()),
            dma(()),
            dma(()),
            dma((2, NCH)),
            dma(()),
            dma((2, NCH)),
            dma(()),
            dma((2, NCH)),
            dma(()),
            dma((NSUP,)),
            dma(()),
            dma((2, NCH)),
            dma(()),
            dma((2, NCH)),
            dma(()),
            dma((NSUP,)),
        ],
        compiler_params=pltpu.CompilerParams(
            collective_id=0, has_side_effects=True, vmem_limit_bytes=60 * 2**20
        ),
    )(ancestor_inverse, panel, pivot_inverse, structure)
    return columns.reshape(32, NSUP, S), diagonal


def solution(mesh):
    return jax.shard_map(
        body,
        mesh=mesh,
        in_specs=(P("prow", "pcol"), P("prow", None, None), P(None, "pcol", "prow"), P()),
        out_specs=(P(("prow", "pcol"), None, None), P(None, "pcol", "prow")),
        check_vma=False,
    )
```

time: 624 us -> 116 us (0.19)
  waiting for transfers between devices: 523 us -> 0 us
  Pallas kernels: 0 us -> 110 us
  matrix products: 32.6 us -> 0 us
  local copies, waits for them, and re-layouts: 28.5 us -> 3.94 us
  other arithmetic: 19.1 us -> 0 us
  between operations: 14.9 us -> 0.64 us
    psum x1 -> x0, waiting for transfers between devices: 185 us -> none  [spread(): return lax.psum(block, axis)]
    unnamed x7 -> x0, waiting for transfers between devices: 162 us -> none
    pallas_call x0 -> x1, Pallas kernels: none -> 110 us  [body(): pl.pallas_call(kernel, name='selinv', out_shape=(jax.ShapeDtypeStruct((32...]
    all_gather x2 -> x0, waiting for transfers between devices: 108 us -> none  [solve_group(): lax.all_gather(solved, 'pcol', axis=0, tiled=True)]
    reduce_scatter x2 -> x0, waiting for transfers between devices: 67.8 us -> none  [solve_group(): lax.psum_scatter(partial_value, 'prow', scatter_dimension=2, tiled=True)]
    dot_general x5 -> x0, matrix products: 32.6 us -> none  [the longest x2 18 us: solve_group(): jnp.dot(ancestor_inverse, flat_panel, precision=lax.Precision.HIGHEST, pr...]
    reshape x2 -> x1, local copies, waits for them, and re-layouts: 22.1 us -> 2.27 us  [body(): return (columns.reshape(32, NSUP, S), diagonal)]
    mul x3 -> x0, other arithmetic: 12.4 us -> none  [the longest x1 8.57 us: body(): masked = lower_panel * row_mask[:, :, None]]
  transfers between devices with their start and end apart: 6 -> 0, of which waited for: 6 -> 0; matrix products, arithmetic and copies ran while one was open for 3% -> 0% of each run, Pallas kernels for 0% -> 0%
where the time goes in v1:
time: 116 us; the launch traced here: 115 us
  Pallas kernels  110 us (95%)
  local copies, waits for them, and re-layouts  3.94 us (3%)
    pallas_call x1, Pallas kernels, body(): pl.pallas_call(kernel, name='selinv', out_shape=(jax.ShapeDtypeStruct((32...  110 us

profile of v1, /device:TPU:1, one launch (start us, length us, event | category | flops | bytes accessed | tf_op | source)
XLA Modules:
  0.0 114.8 jit_solution(17726701651420583867)
XLA Ops:
  0.6 110.2 %selinv.1 = (f32[32,4096]{1,0:T(8,128)}, f32[2,128,256]{2,1,0:T(8,128)}) custom-call(f32[512,256]{1,0:T(8,128)} %a_hbm.1, f32[16384,128]{1,0:T(8,128)} %bitcast.5, f32[2,128,256]{2,1,0:T(8,128)} %piv.1, s32[2,64]{1,0:T(2,128)} %structure.1), custom_call_target="tpu_custom_call" | custom-call | tf_op jit(solution)/shard_map/selinv/pallas_call | solution.py:327
  110.9 2.3 %reshape.15 = f32[32,2,2048]{2,1,0:T(2,128)} reshape(f32[32,4096]{1,0:T(8,128)} %get-tuple-element.4) | data formatting | bytes 1048576 | tf_op jit(solution)/shard_map/reshape | solution.py:375
  113.1 1.7 %copy.8 = f32[2,128,256]{2,1,0:T(8,128)} copy(f32[2,128,256]{2,1,0:T(8,128)} %get-tuple-element.9) | data formatting | bytes 524288

commit v2 on v1

--- a/solution.py
+++ b/solution.py
@@ -33,8 +33,8 @@
 
 def kernel(
     a_hbm, l_hbm, piv, structure, out_c, out_d,
-    lst, xhi, xlo, abuf, ahi, alo, ybuf, zr, xo, xf, cbuf, dbuf, dxo, dxf, dsum, dfin,
-    l_sem, a_send, a_recv, z_send, z_recv, xo_send, xo_recv, xf_send, xf_recv,
+    lst, xhi, xlo, mid, abuf, ahi, alo, ybuf, zr, xo, xf, cbuf, dbuf, dxo, dxf, dsum, dfin,
+    l_sem, m_send, m_recv, a_send, a_recv, z_send, z_recv, xo_send, xo_recv, xf_send, xf_recv,
     c_send, c_recv, dxo_send, dxo_recv, dxf_send, dxf_recv, d_send, d_recv,
 ):
     pr, pc = lax.axis_index("prow"), lax.axis_index("pcol")
@@ -42,10 +42,13 @@
     x, zl = div(pr, 2), rem(pr, 2)
     zh, rest = div(pc, 8), rem(pc, 8)
     z = 2 * zh + zl
-    home, side = div(pc, 2), rem(pc, 2)
+    y, core = div(rest, 2), rem(pc, 2)
 
     def at_z(zz):
         return (x * 2 + rem(zz, 2), div(zz, 2) * 8 + rest)
+
+    def at_xz(xx, zz):
+        return (xx * 2 + rem(zz, 2), div(zz, 2) * 8 + rest)
 
     def at_x(xx):
         return (xx * 2 + zl, pc)
@@ -53,7 +56,6 @@
     z_down, z_up = at_z(rem(z + 3, 4)), at_z(rem(z + 1, 4))
     x_next, x_prev, x_far = rem(x + 1, 4), rem(x + 3, 4), rem(x + 2, 4)
     right, left = at_x(x_next), at_x(x_prev)
-    is_home = home == pr
 
     def remote(src, dst, send, recv, device):
         return pltpu.make_async_remote_copy(
@@ -79,50 +81,16 @@
     def greet(device):
         pl.semaphore_signal(barrier, inc=1, device_id=device, device_id_type=MESH)
 
-    for device in (z_down, z_up, right, left):
-        greet(device)
     for j in range(1, NC):
         greet((pr, rem(pc + j, NC)))
-    for e in range(2):
-        for j in range(1, NR):
-            greet((rem(pr + j, NR), 2 * pr + e))
-
-        @pl.when(2 * pr + e != pc)
-        def _():
-            greet((pr, 2 * pr + e))
-
-    pl.semaphore_wait(barrier, jnp.where(is_home, 34, 35))
-
-    home_zl = rem(home, 2)
-    same = home_zl == zl
-
-    def send_a(j):
-        q = rem(pc + j, NC)
-        z0 = 2 * div(q, 8) + zl
-        for h in range(2):
-            zt = rem(z0 + (1 if h == 0 else 3), 4)
-            qt = jnp.where(same, q, div(zt, 2) * 8 + rem(q, 8))
-            row = jnp.where(same, 128 + x * 32 + h * 16, h * 64 + x * 16)
-            src = a_hbm.at[pl.ds(pl.multiple_of(q * 32 + h * 16, 16), 16)]
-            dst = abuf.at[pl.ds(pl.multiple_of(row, 16), 16), pl.ds(pl.multiple_of(side * 256, 256), 256)]
-            yield src, dst, (home, qt)
-
-    for src, dst, device in send_a(0):
-        @pl.when(is_home)
-        def _():
-            pltpu.make_async_copy(src, dst, a_recv).start()
-
-        @pl.when(jnp.logical_not(is_home))
-        def _():
-            remote(src, dst, a_send, a_recv, device).start()
-
-    @pl.loop(1, NC)
-    def _(j):
-        for src, dst, device in send_a(j):
-            remote(src, dst, a_send, a_recv, device).start()
-
-    @pl.loop(0, NR)
-    def _(i):
+    for j in range(NX):
+        xx = rem(x + j, NX)
+        if j:
+            greet(at_xz(xx, z))
+        greet(at_xz(xx, rem(z + 1, NZ)))
+        greet(at_xz(xx, rem(z + 3, NZ)))
+
+    def prepare(i):
         start = i * rows
         pltpu.make_async_copy(
             l_hbm.at[pl.ds(start, rows)], lst.at[pl.ds(start, rows)], l_sem.at[i]
@@ -135,10 +103,54 @@
                 xhi[k, pl.ds(i * BLK, BLK), pl.ds(col * 128, 128)] = hi
                 xlo[k, pl.ds(i * BLK, BLK), pl.ds(col * 128, 128)] = lo
 
-    await_bytes(abuf, a_recv)
-    hi, lo = split(abuf[...])
-    ahi[...] = hi
-    alo[...] = lo
+    pl.semaphore_wait(barrier, NC - 1 + 3 * NX - 1)
+
+    def a_piece(q):
+        src = a_hbm.at[pl.ds(pl.multiple_of(q * 32, 32), 32)]
+        dst = mid.at[:, pl.ds(pl.multiple_of(pc * 256, 256), 256)]
+        return src, dst
+
+    pltpu.make_async_copy(*a_piece(pc), m_recv.at[div(pc, 2)]).start()
+
+    @pl.loop(1, NC)
+    def _(j):
+        q = rem(pc + j, NC)
+        src, dst = a_piece(q)
+        remote(src, dst, m_send, m_recv.at[div(pc, 2)], (pr, q)).start()
+
+    def forward(target, moved):
+        xx = rem(x + target, NX)
+        tl = 1 - zl if moved else zl
+        column = xx * 2 + tl
+        cols = pl.ds(pl.multiple_of(column * 512, 512), 512)
+        await_bytes(mid.at[:, cols], m_recv.at[column])
+        if moved:
+            for h in range(2):
+                remote(
+                    mid.at[pl.ds(h * 16, 16), cols],
+                    abuf.at[pl.ds(pl.multiple_of(h * 64 + x * 16, 16), 16)],
+                    a_send, a_recv.at[0], at_xz(xx, rem(z + (1 if h == 0 else 3), NZ)),
+                ).start()
+        else:
+            dst = abuf.at[pl.ds(pl.multiple_of(128 + x * 32, 32), 32)]
+            if target:
+                remote(mid.at[:, cols], dst, a_send, a_recv.at[1], at_xz(xx, z)).start()
+            else:
+                pltpu.make_async_copy(mid.at[:, cols], dst, a_recv.at[1]).start()
+
+    @pl.loop(0, 5)
+    def _(i):
+        prepare(i)
+
+    for target in range(NX):
+        forward(target, True)
+
+    for target in range(NX):
+        forward(target, False)
+
+    @pl.loop(5, NR)
+    def _(i):
+        prepare(i)
 
     def z_copies(j):
         cols = pl.ds(pl.multiple_of(j * W, W), W)
@@ -147,14 +159,25 @@
             for h, device in enumerate((z_down, z_up))
         ]
 
-    @pl.loop(0, NCH)
-    def _(j):
-        cols = pl.ds(pl.multiple_of(j * W, W), W)
-        k = div(j, PER_K)
-        kcols = pl.ds(pl.multiple_of(rem(j, PER_K) * W, W), W)
-        ybuf[:, cols] = dot3(ahi[...], alo[...], xhi[k, :, kcols], xlo[k, :, kcols])
-        for copy in z_copies(j):
-            copy.start()
+    def first_product(g):
+        part = pl.ds(g * 128, 128)
+        await_bytes(abuf.at[part], a_recv.at[g])
+        hi, lo = split(abuf[part])
+        ahi[...] = hi
+        alo[...] = lo
+
+        @pl.loop(0, NCH)
+        def _(j):
+            cols = pl.ds(pl.multiple_of(j * W, W), W)
+            k = div(j, PER_K)
+            kcols = pl.ds(pl.multiple_of(rem(j, PER_K) * W, W), W)
+            ybuf[part, cols] = dot3(ahi[...], alo[...], xhi[k, :, kcols], xlo[k, :, kcols])
+            if g == 0:
+                for copy in z_copies(j):
+                    copy.start()
+
+    first_product(0)
+    first_product(1)
 
     def x_stage(buf, row0, far, final, far_send, far_recv, final_send, final_recv):
         def first(j):
@@ -213,10 +236,11 @@
     def finish_c(j):
         cols = pl.ds(pl.multiple_of(j * W, W), W)
         k = div(j, PER_K)
-        mask = structure[k, pr * NR + home].astype(F32)
+        mask = structure[k, pr * NR + div(pc, 2)].astype(F32)
         out_c[:, cols] = -mask * y_total(j)
         for i in range(W // T):
-            q = rem(j, PER_K) * (W // T) + i
+            tx = rem(j, PER_K)
+            q = (i // 2) * 8 + ((i % 2) * 2 + rem(tx + k, 2)) * 2 + div(tx, 2)
             src = out_c.at[:, pl.ds(pl.multiple_of(j * W + i * T, T), T)]
             dst = cbuf.at[k, pl.ds(pl.multiple_of(pc * 32, 32), 32)]
 
@@ -247,8 +271,9 @@
         for i in range(W // T):
             q = rem(j, PER_K) * (W // T) + i
             src = dsum.at[:, pl.ds(pl.multiple_of(j * W + i * T, T), T)]
-            dst = dfin.at[k, zl, pl.ds(pl.multiple_of(side * 128 + x * 32, 32), 32)]
-            own = jnp.logical_and(is_home, q == pc)
+            dst = dfin.at[k, zl, pl.ds(pl.multiple_of(div(y, 2) * 128 + x * 32, 32), 32)]
+            owner = (2 * core + rem(y + k, 2)) * 2 + zh
+            own = jnp.logical_and(owner == pr, q == pc)
 
             @pl.when(own)
             def _():
@@ -256,10 +281,9 @@
 
             @pl.when(jnp.logical_not(own))
             def _():
-                remote(src, dst, d_send, d_recv.at[k], (home, q)).start()
-
-    @pl.loop(0, NCH)
-    def _(j):
+                remote(src, dst, d_send, d_recv.at[k], (owner, q)).start()
+
+    def y_step(j):
         add_z(j)
 
         @pl.when(j >= 1)
@@ -270,20 +294,28 @@
         def _():
             finish_c(j - 2)
 
+    @pl.loop(0, NCH - 1)
+    def _(j):
+        y_step(j)
+
+    second_product(0)
+    add_z(NCH - 1)
+    y_second(NCH - 2)
+    finish_c(NCH - 3)
+
+    @pl.loop(0, PER_K)
+    def _(j):
+        d_second(j)
+
     y_second(NCH - 1)
-    second_product(0)
     finish_c(NCH - 2)
+
+    @pl.loop(0, PER_K)
+    def _(j):
+        finish_d(j)
+
     finish_c(NCH - 1)
-
-    @pl.loop(0, PER_K)
-    def _(j):
-        d_second(j)
-
     second_product(1)
-
-    @pl.loop(0, PER_K)
-    def _(j):
-        finish_d(j)
 
     @pl.loop(PER_K, NCH)
     def _(j):
@@ -297,23 +329,19 @@
         await_bytes(dfin.at[k], d_recv.at[k])
         out_d[k] = piv[k] - (dfin[k, 0] + dfin[k, 1]).T
 
-    await_bytes(abuf.at[pl.ds(0, 240)], a_send)
-
-    @pl.when(jnp.logical_not(is_home))
-    def _():
-        await_bytes(abuf.at[pl.ds(0, 16)], a_send)
-
+    await_bytes(abuf.at[pl.ds(0, 240)], m_send)
+    await_bytes(abuf.at[pl.ds(0, 224)], a_send)
     await_bytes(zr, z_send)
     await_bytes(xo, xo_send)
     await_bytes(xf, xf_send)
     await_bytes(dxo, dxo_send)
     await_bytes(dxf, dxf_send)
     await_bytes(cbuf.at[:, pl.ds(0, 480)], c_send)
-    await_bytes(dfin.at[:, :, pl.ds(0, 240)], d_send)
-
-    @pl.when(jnp.logical_not(is_home))
+    await_bytes(abuf.at[pl.ds(0, 248)], d_send)
+
+    @pl.when(jnp.logical_not(jnp.logical_and(zh == zl, div(x, 2) == core)))
     def _():
-        await_bytes(dfin.at[:, :, pl.ds(0, 16)], d_send)
+        await_bytes(abuf.at[pl.ds(0, 8)], d_send)
 
 
 def body(ancestor_inverse, lower_panel, pivot_inverse, structure):
@@ -337,9 +365,10 @@
             pltpu.VMEM(panel.shape, F32),
             pltpu.VMEM((NSUP, part, S), BF16),
             pltpu.VMEM((NSUP, part, S), BF16),
+            pltpu.VMEM((32, NR * part), F32),
             pltpu.VMEM((256, part), F32),
-            pltpu.VMEM((256, part), BF16),
-            pltpu.VMEM((256, part), BF16),
+            pltpu.VMEM((128, part), BF16),
+            pltpu.VMEM((128, part), BF16),
             pltpu.VMEM((256, width), F32),
             pltpu.VMEM((2, 64, width), F32),
             pltpu.VMEM((2, 16, width), F32),
@@ -352,7 +381,9 @@
             pltpu.VMEM((NSUP, 2, 256, 128), F32),
             dma((NR,)),
             dma(()),
-            dma(()),
+            dma((NR,)),
+            dma(()),
+            dma((2,)),
             dma(()),
             dma((2, NCH)),
             dma(()),

time: 116 us -> 95.7 us (0.83)
  Pallas kernels: 110 us -> 90.9 us
    pallas_call x1, Pallas kernels: 110 us -> 90.9 us  [body(): pl.pallas_call(kernel, name='selinv', out_shape=(jax.ShapeDtypeStruct((32...]
where the time goes in v2:
time: 95.7 us; the launch traced here: 95.5 us
  Pallas kernels  90.9 us (95%)
  local copies, waits for them, and re-layouts  3.94 us (4%)
    pallas_call x1, Pallas kernels, body(): pl.pallas_call(kernel, name='selinv', out_shape=(jax.ShapeDtypeStruct((32...  90.9 us
    reshape x1, local copies, waits for them, and re-layouts, body(): return (columns.reshape(32, NSUP, S), diagonal)  2.27 us

profile of v2, /device:TPU:1, one launch (start us, length us, event | category | flops | bytes accessed | tf_op | source)
XLA Modules:
  0.0 95.5 jit_solution(12310488309445612813)
XLA Ops:
  0.6 90.9 %selinv.1 = (f32[32,4096]{1,0:T(8,128)}, f32[2,128,256]{2,1,0:T(8,128)}) custom-call(f32[512,256]{1,0:T(8,128)} %a_hbm.1, f32[16384,128]{1,0:T(8,128)} %bitcast.5, f32[2,128,256]{2,1,0:T(8,128)} %piv.1, s32[2,64]{1,0:T(2,128)} %structure.1), custom_call_target="tpu_custom_call" | custom-call | tf_op jit(solution)/shard_map/selinv/pallas_call | solution.py:355
  91.6 2.3 %reshape.15 = f32[32,2,2048]{2,1,0:T(2,128)} reshape(f32[32,4096]{1,0:T(8,128)} %get-tuple-element.4) | data formatting | bytes 1048576 | tf_op jit(solution)/shard_map/reshape | solution.py:406
  93.8 1.7 %copy.8 = f32[2,128,256]{2,1,0:T(8,128)} copy(f32[2,128,256]{2,1,0:T(8,128)} %get-tuple-element.9) | data formatting | bytes 524288

commit v3 on v2

--- a/solution.py
+++ b/solution.py
@@ -32,9 +32,9 @@
 
 
 def kernel(
-    a_hbm, l_hbm, piv, structure, out_c, out_d,
-    lst, xhi, xlo, mid, abuf, ahi, alo, ybuf, zr, xo, xf, cbuf, dbuf, dxo, dxf, dsum, dfin,
-    l_sem, m_send, m_recv, a_send, a_recv, z_send, z_recv, xo_send, xo_recv, xf_send, xf_recv,
+    a_hbm, l_hbm, piv_hbm, structure_hbm, out_c, out_d,
+    piv, structure, lst, xhi, xlo, mid, abuf, ahi, alo, ybuf, zr, xo, xf, cbuf, dbuf, dxo, dxf, dsum, dfin,
+    piv_sem, structure_sem, l_sem, m_send, m_recv, a_send, a_recv, z_send, z_recv, xo_send, xo_recv, xf_send, xf_recv,
     c_send, c_recv, dxo_send, dxo_recv, dxf_send, dxf_recv, d_send, d_recv,
 ):
     pr, pc = lax.axis_index("prow"), lax.axis_index("pcol")
@@ -73,8 +73,12 @@
         )
         for i in range(NR)
     ]
+    structure_copy = pltpu.make_async_copy(structure_hbm, structure, structure_sem)
+    structure_copy.start()
     for copy in l_copies:
         copy.start()
+    piv_copy = pltpu.make_async_copy(piv_hbm, piv, piv_sem)
+    piv_copy.start()
 
     barrier = pltpu.get_barrier_semaphore()
 
@@ -138,6 +142,8 @@
             else:
                 pltpu.make_async_copy(mid.at[:, cols], dst, a_recv.at[1]).start()
 
+    structure_copy.wait()
+
     @pl.loop(0, 5)
     def _(i):
         prepare(i)
@@ -298,33 +304,28 @@
     def _(j):
         y_step(j)
 
+    y_step(NCH - 1)
+    y_second(NCH - 1)
     second_product(0)
-    add_z(NCH - 1)
-    y_second(NCH - 2)
-    finish_c(NCH - 3)
+    finish_c(NCH - 2)
+    finish_c(NCH - 1)
 
     @pl.loop(0, PER_K)
     def _(j):
         d_second(j)
 
-    y_second(NCH - 1)
-    finish_c(NCH - 2)
+    second_product(1)
 
     @pl.loop(0, PER_K)
     def _(j):
+        d_second(PER_K + j)
         finish_d(j)
-
-    finish_c(NCH - 1)
-    second_product(1)
-
-    @pl.loop(PER_K, NCH)
-    def _(j):
-        d_second(j)
 
     @pl.loop(PER_K, NCH)
     def _(j):
         finish_d(j)
 
+    piv_copy.wait()
     for k in range(NSUP):
         await_bytes(dfin.at[k], d_recv.at[k])
         out_d[k] = piv[k] - (dfin[k, 0] + dfin[k, 1]).T
@@ -350,7 +351,7 @@
     panel = panel.reshape(part * NSUP * S // 128, 128)
     width = NSUP * S
     vmem = pl.BlockSpec(memory_space=pltpu.VMEM)
-    hbm = pl.BlockSpec(memory_space=pl.ANY)
+    hbm = pl.BlockSpec(memory_space=pltpu.HBM)
     dma = pltpu.SemaphoreType.DMA
     columns, diagonal = pl.pallas_call(
         kernel,
@@ -359,9 +360,11 @@
             jax.ShapeDtypeStruct((32, width), F32),
             jax.ShapeDtypeStruct(pivot_inverse.shape, F32),
         ),
-        in_specs=[hbm, hbm, vmem, pl.BlockSpec(memory_space=pltpu.SMEM)],
+        in_specs=[hbm, hbm, hbm, hbm],
         out_specs=(vmem, vmem),
         scratch_shapes=[
+            pltpu.VMEM(pivot_inverse.shape, F32),
+            pltpu.SMEM(structure.shape, structure.dtype),
             pltpu.VMEM(panel.shape, F32),
             pltpu.VMEM((NSUP, part, S), BF16),
             pltpu.VMEM((NSUP, part, S), BF16),
@@ -379,6 +382,8 @@
             pltpu.VMEM((2, 32, width), F32),
             pltpu.VMEM((32, width), F32),
             pltpu.VMEM((NSUP, 2, 256, 128), F32),
+            dma(()),
+            dma(()),
             dma((NR,)),
             dma(()),
             dma((NR,)),
@@ -400,9 +405,14 @@
             dma((NSUP,)),
         ],
         compiler_params=pltpu.CompilerParams(
-            collective_id=0, has_side_effects=True, vmem_limit_bytes=60 * 2**20
+            collective_id=0, has_side_effects=True, vmem_limit_bytes=40 * 2**20
         ),
-    )(ancestor_inverse, panel, pivot_inverse, structure)
+    )(
+        *(
+            pltpu.with_memory_space_constraint(v, pltpu.HBM)
+            for v in (ancestor_inverse, panel, pivot_inverse, structure)
+        )
+    )
     return columns.reshape(32, NSUP, S), diagonal
 
 

time: 95.7 us -> 87.6 us (0.915)
  the two profiles are of different devices: /device:TPU:1 before, /device:TPU:89 now
where the time goes in v3:
time: 87.6 us; the launch traced here: 87.5 us
  Pallas kernels  84.9 us (97%)
  local copies, waits for them, and re-layouts  1.93 us (2%)
    pallas_call x1, Pallas kernels, body(): pl.pallas_call(kernel, name='selinv', out_shape=(jax.ShapeDtypeStruct((32...  84.9 us

profile of v3, /device:TPU:89, one launch (start us, length us, event | category | flops | bytes accessed | tf_op | source)
XLA Modules:
  0.0 87.5 jit_solution(3697553115252769433)
XLA Ops:
  0.6 84.9 %selinv.1 = (f32[32,4096]{1,0:T(8,128)S(1)}, f32[2,128,256]{2,1,0:T(8,128)S(1)}) custom-call(f32[512,256]{1,0:T(8,128)} %a_hbm.1, f32[16384,128]{1,0:T(8,128)} %bitcast.5, f32[2,128,256]{2,1,0:T(8,128)} %piv_hbm.1, s32[2,64]{1,0:T(2,128)} %structure_hbm.1), custom_call_target="tpu_custom_call" | custom-call | tf_op jit(solution)/shard_map/selinv/pallas_call | solution.py:356
  85.6 1.2 %reshape.15 = f32[32,2,2048]{2,1,0:T(2,128)} reshape(f32[32,4096]{1,0:T(8,128)S(1)} %get-tuple-element.4) | data formatting | bytes 1048576 | tf_op jit(solution)/shard_map/reshape | solution.py:416
  86.8 0.7 copy.8

commit v4 on v0

v4 whole, which is shorter than its diff:
```python
import functools

import jax
import jax.numpy as jnp
from jax import lax
from jax.experimental import pallas as pl
from jax.experimental.pallas import tpu as pltpu
from jax.sharding import PartitionSpec as P

MESH = pl.DeviceIdType.MESH
F32 = jnp.float32
BF16 = jnp.bfloat16
S = 2048
NSUP = 2
BLK = 64
NX, NZ = 4, 4
NR, NC = 8, 16
PART = 512
DEPTH = 2 * PART
W = 512
NCH = S // W
ITEMS = 2 * NCH
EARLY = 4
LAG1, LAG2 = 2, 4
T = S // NC


def split(v):
    hi = v.astype(BF16)
    return hi, (v - hi.astype(F32)).astype(BF16)


def dot3(ahi, alo, bhi, blo):
    dot = functools.partial(jnp.dot, preferred_element_type=F32)
    return dot(ahi, bhi) + (dot(ahi, blo) + dot(alo, bhi))


def kernel(
    a_hbm, l_hbm, piv_hbm, structure_hbm, out_c, out_d,
    piv, structure, lst, xs, xin, xhi, xlo, mid, abuf, ahi, alo, ybuf, xo, xf,
    crow, cout, cbuf, dbuf, dxo, dxf, dsum, dfin,
    piv_sem, structure_sem, l_sem, m_send, m_recv, a_send, a_recv, n_send, n_recv,
    x_send, x_recv, p_send, p_recv, xo_send, xo_recv, xf_send, xf_recv,
    c_send, c_recv, o_send, o_recv, dxo_send, dxo_recv, dxf_send, dxf_recv, d_send, d_recv,
):
    rem, div = lax.rem, lax.div
    pr, pc = lax.axis_index("prow"), lax.axis_index("pcol")
    x, zl = div(pr, 2), rem(pr, 2)
    zh, rest = div(pc, 8), rem(pc, 8)
    y, core = div(rest, 2), rem(pc, 2)
    z = 2 * zh + zl
    other = 1 - zl

    def at_xz(xx, zz):
        return (xx * 2 + rem(zz, 2), div(zz, 2) * 8 + rest)

    z_down, z_up = at_xz(x, rem(z + 3, 4)), at_xz(x, rem(z + 1, 4))
    x_next, x_prev, x_far = rem(x + 1, 4), rem(x + 3, 4), rem(x + 2, 4)
    right, left = at_xz(x_next, z), at_xz(x_prev, z)
    partner = (pr, pc + 1 - 2 * core)

    def remote(src, dst, send, recv, device):
        return pltpu.make_async_remote_copy(
            src_ref=src, dst_ref=dst, send_sem=send, recv_sem=recv,
            device_id=device, device_id_type=MESH,
        )

    def await_bytes(ref, sem):
        pltpu.make_async_copy(ref, ref, sem).wait()

    def span(start, size):
        return pl.ds(pl.multiple_of(start, size), size)

    rows = BLK * NSUP * S // 128
    structure_copy = pltpu.make_async_copy(structure_hbm, structure, structure_sem)
    structure_copy.start()
    for i in range(NR):
        block = pl.ds(i * rows, rows)
        pltpu.make_async_copy(l_hbm.at[block], lst.at[block], l_sem.at[i]).start()
    piv_copy = pltpu.make_async_copy(piv_hbm, piv, piv_sem)
    piv_copy.start()

    barrier = pltpu.get_barrier_semaphore()

    def greet(device):
        pl.semaphore_signal(barrier, inc=1, device_id=device, device_id_type=MESH)

    for j in range(1, NC):
        greet((pr, rem(pc + j, NC)))
    for j in range(1, NX):
        greet(at_xz(rem(x + j, NX), z))
    greet(z_down)
    greet(z_up)
    pl.semaphore_wait(barrier, NC - 1 + NX - 1 + 2)

    def a_piece(q):
        src = a_hbm.at[span(q * 32, 32)]
        return src, mid.at[:, span(pc * 256, 256)], m_recv.at[div(pc, 4)]

    pltpu.make_async_copy(*a_piece(pc)).start()

    @pl.loop(1, NC)
    def _(j):
        q = rem(pc + j, NC)
        src, dst, recv = a_piece(q)
        remote(src, dst, m_send, recv, (pr, q)).start()

    structure_copy.wait()
    for i in range(NR):
        block = pl.ds(i * rows, rows)
        pltpu.make_async_copy(l_hbm.at[block], lst.at[block], l_sem.at[i]).wait()

    def pack(j):
        for part in range(2):
            for b in range(2):
                i = part * 4 + 2 * core + b
                mask = structure[other, pr * NR + i].astype(F32)
                for col in range(W // 128):
                    first = i * rows + (j * (W // 128) + col) * NSUP + other
                    v = lst[pl.ds(first, BLK, stride=S * NSUP // 128), :]
                    xs[pl.ds(part * 128 + b * BLK, BLK), span((j * (W // 128) + col) * 128, 128)] = v * mask

    def x_copies(j):
        cols = span(j * W, W)
        return [
            remote(
                xs.at[pl.ds(part * 128, 128), cols],
                xin.at[span(part * 256 + core * 128, 128), cols],
                x_send, x_recv.at[part, j], device,
            )
            for part, device in enumerate((z_up, z_down))
        ]

    def send_x(j):
        for copy in x_copies(j):
            copy.start()

    def p_copies(j):
        cols = span(j * W, W)
        return [
            remote(
                xin.at[span(part * 256 + core * 128, 128), cols],
                xin.at[span(part * 256 + core * 128, 128), cols],
                p_send, p_recv.at[part, j], partner,
            )
            for part in range(2)
        ]

    def relay(j):
        for arrived, copy in zip(x_copies(j), p_copies(j)):
            arrived.wait_recv()
            copy.start()

    def take(j):
        for copy in p_copies(j):
            copy.wait_recv()
        cols = span(j * W, W)
        hi, lo = split(xin[:, cols])
        xhi[span(other * PART, PART), cols] = hi
        xlo[span(other * PART, PART), cols] = lo

    def prepare(i):
        mask = structure[zl, pr * NR + i].astype(F32)
        for col in range(S // 128):
            v = lst[pl.ds(i * rows + col * NSUP + zl, BLK, stride=S * NSUP // 128), :] * mask
            hi, lo = split(v)
            block = span(zl * PART + i * BLK, BLK)
            xhi[block, pl.ds(col * 128, 128)] = hi
            xlo[block, pl.ds(col * 128, 128)] = lo

    def forward(j):
        xx = rem(x + j, NX)
        cols = span(xx * DEPTH, DEPTH)
        await_bytes(mid.at[:, cols], m_recv.at[xx])
        dst = abuf.at[0, span(x * 32, 32)]
        if j:
            remote(mid.at[:, cols], dst, a_send, a_recv.at[x], at_xz(xx, z)).start()
        else:
            pltpu.make_async_copy(mid.at[:, cols], dst, a_recv.at[x]).start()

    def share(xx):
        await_bytes(abuf.at[0, span(xx * 32, 32)], a_recv.at[xx])
        for h, device in enumerate((z_up, z_down)):
            block = span(xx * 32 + h * 16, 16)
            remote(abuf.at[0, block], abuf.at[1, block], n_send, n_recv, device).start()

    def split_rows(g):
        hi, lo = split(abuf[g])
        ahi[g] = hi
        alo[g] = lo

    pack(0)
    send_x(0)

    @pl.loop(1, NCH)
    def _(j):
        pack(j)

    @pl.loop(0, EARLY)
    def _(i):
        prepare(i)

    for j in (1, 2, 3, 0):
        forward(j)
    send_x(1)

    @pl.loop(EARLY, NR)
    def _(i):
        prepare(i)

    relay(0)
    for j in (0, 1, 3, 2):
        share(rem(x + j, NX))
    send_x(2)
    send_x(3)
    relay(1)
    split_rows(0)

    def x_stage(buf, far, final, far_send, far_recv, final_send, final_recv):
        def first(j):
            cols = span(j * W, W)
            return [
                remote(
                    buf.at[span(x_far * 32 + h * 16, 16), cols],
                    far.at[h, :, cols], far_send, far_recv.at[h, j], device,
                )
                for h, device in enumerate((right, left))
            ]

        def second(j):
            cols = span(j * W, W)
            return [
                remote(
                    buf.at[span(target * 32, 32), cols],
                    final.at[h, :, cols], final_send, final_recv.at[h, j], device,
                )
                for h, (device, target) in enumerate(((right, x_next), (left, x_prev)))
            ]

        def send_first(j):
            for copy in first(j):
                copy.start()

        def send_second(j):
            cols = span(j * W, W)
            for h, (copy, target) in enumerate(zip(first(j), (x_next, x_prev))):
                copy.wait_recv()
                buf[span(target * 32 + h * 16, 16), cols] += far[h, :, cols]
            for copy in second(j):
                copy.start()

        def total(j):
            cols = span(j * W, W)
            for copy in second(j):
                copy.wait_recv()
            return buf[span(x * 32, 32), cols] + (final[0, :, cols] + final[1, :, cols])

        return send_first, send_second, total

    y_first, y_second, y_total = x_stage(ybuf, xo, xf, xo_send, xo_recv, xf_send, xf_recv)
    d_first, d_second, d_total = x_stage(dbuf, dxo, dxf, dxo_send, dxo_recv, dxf_send, dxf_recv)

    def item(i):
        g = jnp.where(i < 4, div(i, 2), rem(i, 2))
        c = jnp.where(i < 4, rem(i, 2), div(i, 2))
        return g, c, g * NCH + c

    def first_product(i):
        g, c, j = item(i)
        cols = span(c * W, W)
        ybuf[:, span(j * W, W)] = dot3(ahi[g], alo[g], xhi[:, cols], xlo[:, cols])
        y_first(j)

    def finish_c(i):
        g, c, j = item(i)
        cols = span(j * W, W)
        value = y_total(j)
        for h, neighbour in enumerate((z_down, z_up)):
            owner_row = jnp.where(g == 0, pr, neighbour[0])
            owner_col = jnp.where(g == 0, pc, neighbour[1])
            mask = structure[zl, owner_row * NR + div(owner_col, 2)].astype(F32)
            part = pl.ds(h * 16, 16)
            crow[part, cols] = -mask * value[h * 16 : h * 16 + 16]
            home = span(rem(owner_row, 2) * PART + owner_col * 32 + h * 16, 16)
            for n in range(W // T):
                q = (n // 2) * 8 + ((n % 2) * 2 + rem(c + n // 2, 2)) * 2 + div(c, 2)
                src = crow.at[part, span(j * W + n * T, T)]

                @pl.when(q == pc)
                def _():
                    pltpu.make_async_copy(src, cbuf.at[home], c_recv).start()

                @pl.when(q != pc)
                def _():
                    remote(src, cbuf.at[home], c_send, c_recv, (pr, q)).start()

            @pl.when(g == 1)
            def _():
                remote(crow.at[part, cols], cout.at[part, span(c * W, W)], o_send, o_recv, neighbour).start()

        @pl.when(g == 0)
        def _():
            out_c[:, span(zl * S + c * W, W)] = crow[:, cols]

    @pl.loop(0, ITEMS + LAG2)
    def _(i):
        @pl.when(jnp.logical_or(i < 2, jnp.logical_or(i == 4, i == 6)))
        def _():
            take(jnp.where(i < 2, i, div(i, 2)))

        @pl.when(i == 2)
        def _():
            await_bytes(abuf.at[1], n_recv)
            split_rows(1)

        @pl.when(i < ITEMS)
        def _():
            first_product(i)

        @pl.when(jnp.logical_or(i == 3, i == 5))
        def _():
            relay(div(i, 2) + 1)

        @pl.when(jnp.logical_and(i >= LAG1, i < ITEMS + LAG1))
        def _():
            y_second(item(i - LAG1)[2])

        @pl.when(i >= LAG2)
        def _():
            finish_c(i - LAG2)

    await_bytes(cbuf, c_recv)
    chi, clo = split(cbuf[...].T)

    @pl.loop(0, NCH)
    def _(n):
        cols = span(n * W, W)
        dbuf[:, cols] = dot3(chi, clo, xhi[:, cols], xlo[:, cols])
        d_first(n)

    @pl.loop(0, NCH)
    def _(n):
        d_second(n)

    owner = (2 * core + rem(y + zh, 2)) * 2 + zh

    @pl.loop(0, NCH)
    def _(n):
        dsum[:, span(n * W, W)] = d_total(n)
        for i in range(W // T):
            q = n * (W // T) + i
            src = dsum.at[:, span(q * T, T)]
            dst = dfin.at[zl, span(div(y, 2) * 128 + x * 32, 32)]
            own = jnp.logical_and(owner == pr, q == pc)

            @pl.when(own)
            def _():
                pltpu.make_async_copy(src, dst, d_recv).start()

            @pl.when(jnp.logical_not(own))
            def _():
                remote(src, dst, d_send, d_recv, (owner, q)).start()

    await_bytes(cout, o_recv)
    out_c[:, span(other * S, S)] = cout[...]
    piv_copy.wait()
    await_bytes(dfin, d_recv)
    for k in range(NSUP):
        out_d[k] = piv[k] - dfin[k].T

    await_bytes(abuf.at[0, pl.ds(0, 120)], m_send)
    await_bytes(abuf.at[0, pl.ds(0, 96)], a_send)
    await_bytes(abuf.at[0], n_send)
    await_bytes(xs, x_send)
    await_bytes(xs, p_send)
    await_bytes(xo, xo_send)
    await_bytes(xf, xf_send)
    await_bytes(cbuf.at[pl.ds(0, 960)], c_send)
    await_bytes(cout, o_send)
    await_bytes(dxo, dxo_send)
    await_bytes(dxf, dxf_send)
    await_bytes(cbuf.at[pl.ds(0, 480)], d_send)

    @pl.when(owner != pr)
    def _():
        await_bytes(cbuf.at[pl.ds(0, 32)], d_send)


def body(ancestor_inverse, lower_panel, pivot_inverse, structure):
    panel = lower_panel.reshape(PART, NSUP, S // 128, 128).transpose(0, 2, 1, 3)
    panel = panel.reshape(PART * NSUP * S // 128, 128)
    width = NSUP * S
    vmem = pl.BlockSpec(memory_space=pltpu.VMEM)
    hbm = pl.BlockSpec(memory_space=pltpu.HBM)
    dma = pltpu.SemaphoreType.DMA
    columns, diagonal = pl.pallas_call(
        kernel,
        name="selinv",
        out_shape=(
            jax.ShapeDtypeStruct((32, width), F32),
            jax.ShapeDtypeStruct(pivot_inverse.shape, F32),
        ),
        in_specs=[hbm, hbm, hbm, hbm],
        out_specs=(vmem, vmem),
        scratch_shapes=[
            pltpu.VMEM(pivot_inverse.shape, F32),
            pltpu.SMEM(structure.shape, structure.dtype),
            pltpu.VMEM(panel.shape, F32),
            pltpu.VMEM((256, S), F32),
            pltpu.VMEM((PART, S), F32),
            pltpu.VMEM((DEPTH, S), BF16),
            pltpu.VMEM((DEPTH, S), BF16),
            pltpu.VMEM((32, NX * DEPTH), F32),
            pltpu.VMEM((2, 128, DEPTH), F32),
            pltpu.VMEM((2, 128, DEPTH), BF16),
            pltpu.VMEM((2, 128, DEPTH), BF16),
            pltpu.VMEM((128, width), F32),
            pltpu.VMEM((2, 16, width), F32),
            pltpu.VMEM((2, 32, width), F32),
            pltpu.VMEM((32, width), F32),
            pltpu.VMEM((32, S), F32),
            pltpu.VMEM((DEPTH, T), F32),
            pltpu.VMEM((128, S), F32),
            pltpu.VMEM((2, 16, S), F32),
            pltpu.VMEM((2, 32, S), F32),
            pltpu.VMEM((32, S), F32),
            pltpu.VMEM((NSUP, 256, 128), F32),
            dma(()),
            dma(()),
            dma((NR,)),
            dma(()),
            dma((NX,)),
            dma(()),
            dma((NX,)),
            dma(()),
            dma(()),
            dma(()),
            dma((2, NCH)),
            dma(()),
            dma((2, NCH)),
            dma(()),
            dma((2, ITEMS)),
            dma(()),
            dma((2, ITEMS)),
            dma(()),
            dma(()),
            dma(()),
            dma(()),
            dma(()),
            dma((2, NCH)),
            dma(()),
            dma((2, NCH)),
            dma(()),
            dma(()),
        ],
        compiler_params=pltpu.CompilerParams(
            collective_id=0, has_side_effects=True, vmem_limit_bytes=40 * 2**20
        ),
    )(
        *(
            pltpu.with_memory_space_constraint(v, pltpu.HBM)
            for v in (ancestor_inverse, panel, pivot_inverse, structure)
        )
    )
    return columns.reshape(32, NSUP, S), diagonal


def solution(mesh):
    return jax.shard_map(
        body,
        mesh=mesh,
        in_specs=(P("prow", "pcol"), P("prow", None, None), P(None, "pcol", "prow"), P()),
        out_specs=(P(("prow", "pcol"), None, None), P(None, "pcol", "prow")),
        check_vma=False,
    )
```

time: 624 us -> 79.1 us (0.13)
  waiting for transfers between devices: 523 us -> 0 us
  Pallas kernels: 0 us -> 75.7 us
  matrix products: 32.6 us -> 0 us
  local copies, waits for them, and re-layouts: 28.5 us -> 1.93 us
  other arithmetic: 19.1 us -> 0 us
  between operations: 14.9 us -> 0.64 us
    psum x1 -> x0, waiting for transfers between devices: 185 us -> none  [spread(): return lax.psum(block, axis)]
    unnamed x7 -> x0, waiting for transfers between devices: 162 us -> none
    all_gather x2 -> x0, waiting for transfers between devices: 108 us -> none  [solve_group(): lax.all_gather(solved, 'pcol', axis=0, tiled=True)]
    pallas_call x0 -> x1, Pallas kernels: none -> 75.7 us  [body(): pl.pallas_call(kernel, name='selinv', out_shape=(jax.ShapeDtypeStruct((32...]
    reduce_scatter x2 -> x0, waiting for transfers between devices: 67.8 us -> none  [solve_group(): lax.psum_scatter(partial_value, 'prow', scatter_dimension=2, tiled=True)]
    dot_general x5 -> x0, matrix products: 32.6 us -> none  [the longest x2 18 us: solve_group(): jnp.dot(ancestor_inverse, flat_panel, precision=lax.Precision.HIGHEST, pr...]
    reshape x2 -> x1, local copies, waits for them, and re-layouts: 22.1 us -> 1.23 us  [body(): return (columns.reshape(32, NSUP, S), diagonal)]
    mul x3 -> x0, other arithmetic: 12.4 us -> none  [the longest x1 8.57 us: body(): masked = lower_panel * row_mask[:, :, None]]
  transfers between devices with their start and end apart: 6 -> 0, of which waited for: 6 -> 0; matrix products, arithmetic and copies ran while one was open for 3% -> 0% of each run, Pallas kernels for 0% -> 0%
where the time goes in v4:
time: 79.1 us; the launch traced here: 78.3 us
  Pallas kernels  75.7 us (96%)
  local copies, waits for them, and re-layouts  1.93 us (2%)
    pallas_call x1, Pallas kernels, body(): pl.pallas_call(kernel, name='selinv', out_shape=(jax.ShapeDtypeStruct((32...  75.7 us

profile of v4, /device:TPU:1, one launch (start us, length us, event | category | flops | bytes accessed | tf_op | source)
XLA Modules:
  0.0 78.3 jit_solution(15495668344779567360)
XLA Ops:
  0.6 75.7 %selinv.1 = (f32[32,4096]{1,0:T(8,128)S(1)}, f32[2,128,256]{2,1,0:T(8,128)S(1)}) custom-call(f32[512,256]{1,0:T(8,128)} %a_hbm.1, f32[16384,128]{1,0:T(8,128)} %bitcast.5, f32[2,128,256]{2,1,0:T(8,128)} %piv_hbm.1, s32[2,64]{1,0:T(2,128)} %structure_hbm.1), custom_call_target="tpu_custom_call" | custom-call | tf_op jit(solution)/shard_map/selinv/pallas_call | solution.py:396
  76.3 1.2 %reshape.15 = f32[32,2,2048]{2,1,0:T(2,128)} reshape(f32[32,4096]{1,0:T(8,128)S(1)} %get-tuple-element.4) | data formatting | bytes 1048576 | tf_op jit(solution)/shard_map/reshape | solution.py:465
  77.6 0.7 copy.8

commit v5 on v4

--- a/solution.py
+++ b/solution.py
@@ -22,6 +22,7 @@
 ITEMS = 2 * NCH
 EARLY = 4
 LAG1, LAG2 = 2, 4
+DIAG = 12
 T = S // NC
 
 
@@ -40,7 +41,7 @@
     piv, structure, lst, xs, xin, xhi, xlo, mid, abuf, ahi, alo, ybuf, xo, xf,
     crow, cout, cbuf, dbuf, dxo, dxf, dsum, dfin,
     piv_sem, structure_sem, l_sem, m_send, m_recv, a_send, a_recv, n_send, n_recv,
-    x_send, x_recv, p_send, p_recv, xo_send, xo_recv, xf_send, xf_recv,
+    x_send, x_recv, w_send, p_send, p_recv, xo_send, xo_recv, xf_send, xf_recv,
     c_send, c_recv, o_send, o_recv, dxo_send, dxo_recv, dxf_send, dxf_recv, d_send, d_recv,
 ):
     rem, div = lax.rem, lax.div
@@ -58,6 +59,11 @@
     x_next, x_prev, x_far = rem(x + 1, 4), rem(x + 3, 4), rem(x + 2, 4)
     right, left = at_xz(x_next, z), at_xz(x_prev, z)
     partner = (pr, pc + 1 - 2 * core)
+    y_up, y_down = ((pr, zh * 8 + rem(y + d, 4) * 2 + core) for d in (1, 3))
+    parity = rem(y, 2)
+
+    def chunk(n):
+        return n + parity * (1 - 2 * rem(n, 2))
 
     def remote(src, dst, send, recv, device):
         return pltpu.make_async_remote_copy(
@@ -146,9 +152,13 @@
             for part in range(2)
         ]
 
-    def relay(j):
-        for arrived, copy in zip(x_copies(j), p_copies(j)):
+    def relay(j, pass_on):
+        cols = span(j * W, W)
+        for part, (arrived, copy) in enumerate(zip(x_copies(j), p_copies(j))):
             arrived.wait_recv()
+            if pass_on:
+                block = xin.at[span(part * 256 + core * 128, 128), cols]
+                remote(block, block, w_send, x_recv.at[part, j], (y_up, y_down)[part]).start()
             copy.start()
 
     def take(j):
@@ -189,12 +199,9 @@
         ahi[g] = hi
         alo[g] = lo
 
-    pack(0)
-    send_x(0)
-
-    @pl.loop(1, NCH)
-    def _(j):
-        pack(j)
+    for n in (0, 2):
+        pack(chunk(n))
+        send_x(chunk(n))
 
     @pl.loop(0, EARLY)
     def _(i):
@@ -202,18 +209,14 @@
 
     for j in (1, 2, 3, 0):
         forward(j)
-    send_x(1)
 
     @pl.loop(EARLY, NR)
     def _(i):
         prepare(i)
 
-    relay(0)
+    relay(chunk(0), True)
     for j in (0, 1, 3, 2):
         share(rem(x + j, NX))
-    send_x(2)
-    send_x(3)
-    relay(1)
     split_rows(0)
 
     def x_stage(buf, far, final, far_send, far_recv, final_send, final_recv):
@@ -261,8 +264,10 @@
     d_first, d_second, d_total = x_stage(dbuf, dxo, dxf, dxo_send, dxo_recv, dxf_send, dxf_recv)
 
     def item(i):
-        g = jnp.where(i < 4, div(i, 2), rem(i, 2))
-        c = jnp.where(i < 4, rem(i, 2), div(i, 2))
+        own = jnp.logical_or(i < 3, i == 5)
+        g = jnp.where(own, 0, 1)
+        n = jnp.where(i < 3, rem(2 * i, 3), jnp.where(i < 5, i - 3, jnp.where(i == 5, 3, i - 4)))
+        c = chunk(n)
         return g, c, g * NCH + c
 
     def first_product(i):
@@ -302,13 +307,32 @@
         def _():
             out_c[:, span(zl * S + c * W, W)] = crow[:, cols]
 
-    @pl.loop(0, ITEMS + LAG2)
+    def turned(n):
+        return rem(n + y, NCH)
+
+    def second_product():
+        await_bytes(cbuf, c_recv)
+        chi, clo = split(cbuf[...].T)
+
+        @pl.loop(0, NCH)
+        def _(i):
+            n = turned(i)
+            cols = span(n * W, W)
+            dbuf[:, cols] = dot3(chi, clo, xhi[:, cols], xlo[:, cols])
+            d_first(n)
+
+    def second_ring():
+        @pl.loop(0, NCH)
+        def _(n):
+            d_second(turned(n))
+
+    @pl.loop(0, 14)
     def _(i):
-        @pl.when(jnp.logical_or(i < 2, jnp.logical_or(i == 4, i == 6)))
-        def _():
-            take(jnp.where(i < 2, i, div(i, 2)))
-
-        @pl.when(i == 2)
+        @pl.when(jnp.logical_or(i < 3, i == 5))
+        def _():
+            take(item(i)[1])
+
+        @pl.when(i == 3)
         def _():
             await_bytes(abuf.at[1], n_recv)
             split_rows(1)
@@ -317,35 +341,40 @@
         def _():
             first_product(i)
 
-        @pl.when(jnp.logical_or(i == 3, i == 5))
-        def _():
-            relay(div(i, 2) + 1)
+        @pl.when(i == 0)
+        def _():
+            relay(chunk(2), True)
+
+        @pl.when(jnp.logical_or(i == 1, i == 3))
+        def _():
+            relay(chunk(i), False)
 
         @pl.when(jnp.logical_and(i >= LAG1, i < ITEMS + LAG1))
         def _():
             y_second(item(i - LAG1)[2])
 
-        @pl.when(i >= LAG2)
+        @pl.when(jnp.logical_and(i >= LAG2, i < ITEMS + LAG2))
         def _():
             finish_c(i - LAG2)
 
-    await_bytes(cbuf, c_recv)
-    chi, clo = split(cbuf[...].T)
+        @pl.when(jnp.logical_and(i == DIAG, core == 0))
+        def _():
+            second_product()
+
+        @pl.when(jnp.logical_and(i == DIAG + 1, core == 0))
+        def _():
+            second_ring()
+
+    @pl.when(core == 1)
+    def _():
+        second_product()
+        second_ring()
+
+    owner = (2 * core + rem(y + zh, 2)) * 2 + zh
 
     @pl.loop(0, NCH)
-    def _(n):
-        cols = span(n * W, W)
-        dbuf[:, cols] = dot3(chi, clo, xhi[:, cols], xlo[:, cols])
-        d_first(n)
-
-    @pl.loop(0, NCH)
-    def _(n):
-        d_second(n)
-
-    owner = (2 * core + rem(y + zh, 2)) * 2 + zh
-
-    @pl.loop(0, NCH)
-    def _(n):
+    def _(j):
+        n = turned(j)
         dsum[:, span(n * W, W)] = d_total(n)
         for i in range(W // T):
             q = n * (W // T) + i
@@ -371,7 +400,8 @@
     await_bytes(abuf.at[0, pl.ds(0, 120)], m_send)
     await_bytes(abuf.at[0, pl.ds(0, 96)], a_send)
     await_bytes(abuf.at[0], n_send)
-    await_bytes(xs, x_send)
+    await_bytes(xs.at[pl.ds(0, 128)], x_send)
+    await_bytes(xs.at[pl.ds(0, 128)], w_send)
     await_bytes(xs, p_send)
     await_bytes(xo, xo_send)
     await_bytes(xf, xf_send)
@@ -437,6 +467,7 @@
             dma(()),
             dma((2, NCH)),
             dma(()),
+            dma(()),
             dma((2, NCH)),
             dma(()),
             dma((2, ITEMS)),

time: 79.1 us -> 75.3 us (0.952)
  Pallas kernels: 75.7 us -> 72.6 us
    pallas_call x1, Pallas kernels: 75.7 us -> 72.6 us  [body(): pl.pallas_call(kernel, name='selinv', out_shape=(jax.ShapeDtypeStruct((32...]
where the time goes in v5:
time: 75.3 us; the launch traced here: 75.1 us
  Pallas kernels  72.6 us (96%)
  local copies, waits for them, and re-layouts  1.93 us (3%)
    pallas_call x1, Pallas kernels, body(): pl.pallas_call(kernel, name='selinv', out_shape=(jax.ShapeDtypeStruct((32...  72.6 us

profile of v5, /device:TPU:1, one launch (start us, length us, event | category | flops | bytes accessed | tf_op | source)
XLA Modules:
  0.0 75.1 jit_solution(11392169574048266464)
XLA Ops:
  0.6 72.6 %selinv.1 = (f32[32,4096]{1,0:T(8,128)S(1)}, f32[2,128,256]{2,1,0:T(8,128)S(1)}) custom-call(f32[512,256]{1,0:T(8,128)} %a_hbm.1, f32[16384,128]{1,0:T(8,128)} %bitcast.5, f32[2,128,256]{2,1,0:T(8,128)} %piv_hbm.1, s32[2,64]{1,0:T(2,128)} %structure_hbm.1), custom_call_target="tpu_custom_call" | custom-call | tf_op jit(solution)/shard_map/selinv/pallas_call | solution.py:426
  73.2 1.2 %reshape.15 = f32[32,2,2048]{2,1,0:T(2,128)} reshape(f32[32,4096]{1,0:T(8,128)S(1)} %get-tuple-element.4) | data formatting | bytes 1048576 | tf_op jit(solution)/shard_map/reshape | solution.py:496
  74.4 0.7 copy.8

commit v6 on v5

--- a/solution.py
+++ b/solution.py
@@ -20,9 +20,9 @@
 W = 512
 NCH = S // W
 ITEMS = 2 * NCH
-EARLY = 4
+EARLY = 5
 LAG1, LAG2 = 2, 4
-DIAG = 12
+H = W // 2
 T = S // NC
 
 
@@ -99,17 +99,18 @@
     greet(z_up)
     pl.semaphore_wait(barrier, NC - 1 + NX - 1 + 2)
 
-    def a_piece(q):
-        src = a_hbm.at[span(q * 32, 32)]
-        return src, mid.at[:, span(pc * 256, 256)], m_recv.at[div(pc, 4)]
-
-    pltpu.make_async_copy(*a_piece(pc)).start()
-
-    @pl.loop(1, NC)
-    def _(j):
-        q = rem(pc + j, NC)
-        src, dst, recv = a_piece(q)
-        remote(src, dst, m_send, recv, (pr, q)).start()
+    def a_piece(q, h):
+        src = a_hbm.at[span(q * 32 + h * 16, 16)]
+        return src, mid.at[pl.ds(h * 16, 16), span(pc * 256, 256)], m_recv.at[h, div(pc, 4)]
+
+    for h in range(2):
+        pltpu.make_async_copy(*a_piece(pc, h)).start()
+
+        @pl.loop(1, NC)
+        def _(j):
+            q = rem(pc + j, NC)
+            src, dst, recv = a_piece(q, h)
+            remote(src, dst, m_send, recv, (pr, q)).start()
 
     structure_copy.wait()
     for i in range(NR):
@@ -126,44 +127,46 @@
                     v = lst[pl.ds(first, BLK, stride=S * NSUP // 128), :]
                     xs[pl.ds(part * 128 + b * BLK, BLK), span((j * (W // 128) + col) * 128, 128)] = v * mask
 
-    def x_copies(j):
-        cols = span(j * W, W)
+    def x_copies(j, half):
+        cols = span(j * W + half * H, H)
         return [
             remote(
                 xs.at[pl.ds(part * 128, 128), cols],
                 xin.at[span(part * 256 + core * 128, 128), cols],
-                x_send, x_recv.at[part, j], device,
+                x_send, x_recv.at[part, 2 * j + half], device,
             )
             for part, device in enumerate((z_up, z_down))
         ]
 
     def send_x(j):
-        for copy in x_copies(j):
-            copy.start()
-
-    def p_copies(j):
-        cols = span(j * W, W)
+        for half in range(2):
+            for copy in x_copies(j, half):
+                copy.start()
+
+    def p_copies(j, half):
+        cols = span(j * W + half * H, H)
         return [
             remote(
                 xin.at[span(part * 256 + core * 128, 128), cols],
                 xin.at[span(part * 256 + core * 128, 128), cols],
-                p_send, p_recv.at[part, j], partner,
+                p_send, p_recv.at[part, 2 * j + half], partner,
             )
             for part in range(2)
         ]
 
-    def relay(j, pass_on):
-        cols = span(j * W, W)
-        for part, (arrived, copy) in enumerate(zip(x_copies(j), p_copies(j))):
+    def relay(j, half, pass_on):
+        cols = span(j * W + half * H, H)
+        for part, (arrived, copy) in enumerate(zip(x_copies(j, half), p_copies(j, half))):
             arrived.wait_recv()
             if pass_on:
                 block = xin.at[span(part * 256 + core * 128, 128), cols]
-                remote(block, block, w_send, x_recv.at[part, j], (y_up, y_down)[part]).start()
+                remote(block, block, w_send, x_recv.at[part, 2 * j + half], (y_up, y_down)[part]).start()
             copy.start()
 
     def take(j):
-        for copy in p_copies(j):
-            copy.wait_recv()
+        for half in range(2):
+            for copy in p_copies(j, half):
+                copy.wait_recv()
         cols = span(j * W, W)
         hi, lo = split(xin[:, cols])
         xhi[span(other * PART, PART), cols] = hi
@@ -178,21 +181,23 @@
             xhi[block, pl.ds(col * 128, 128)] = hi
             xlo[block, pl.ds(col * 128, 128)] = lo
 
-    def forward(j):
-        xx = rem(x + j, NX)
-        cols = span(xx * DEPTH, DEPTH)
-        await_bytes(mid.at[:, cols], m_recv.at[xx])
-        dst = abuf.at[0, span(x * 32, 32)]
-        if j:
-            remote(mid.at[:, cols], dst, a_send, a_recv.at[x], at_xz(xx, z)).start()
-        else:
-            pltpu.make_async_copy(mid.at[:, cols], dst, a_recv.at[x]).start()
-
-    def share(xx):
-        await_bytes(abuf.at[0, span(xx * 32, 32)], a_recv.at[xx])
-        for h, device in enumerate((z_up, z_down)):
+    def forward(h):
+        for j in (1, 2, 3, 0):
+            xx = rem(x + j, NX)
+            src = mid.at[pl.ds(h * 16, 16), span(xx * DEPTH, DEPTH)]
+            await_bytes(src, m_recv.at[h, xx])
+            dst, recv = abuf.at[0, span(x * 32 + h * 16, 16)], a_recv.at[h, x]
+            if j:
+                remote(src, dst, a_send, recv, at_xz(xx, z)).start()
+            else:
+                pltpu.make_async_copy(src, dst, recv).start()
+
+    def share(h):
+        for j in (0, 1, 3, 2):
+            xx = rem(x + j, NX)
             block = span(xx * 32 + h * 16, 16)
-            remote(abuf.at[0, block], abuf.at[1, block], n_send, n_recv, device).start()
+            await_bytes(abuf.at[0, block], a_recv.at[h, xx])
+            remote(abuf.at[0, block], abuf.at[1, block], n_send, n_recv, (z_up, z_down)[h]).start()
 
     def split_rows(g):
         hi, lo = split(abuf[g])
@@ -207,16 +212,17 @@
     def _(i):
         prepare(i)
 
-    for j in (1, 2, 3, 0):
-        forward(j)
+    forward(0)
 
     @pl.loop(EARLY, NR)
     def _(i):
         prepare(i)
 
-    relay(chunk(0), True)
-    for j in (0, 1, 3, 2):
-        share(rem(x + j, NX))
+    forward(1)
+    share(0)
+    relay(chunk(0), 0, True)
+    share(1)
+    relay(chunk(0), 1, True)
     split_rows(0)
 
     def x_stage(buf, far, final, far_send, far_recv, final_send, final_recv):
@@ -293,11 +299,11 @@
 
                 @pl.when(q == pc)
                 def _():
-                    pltpu.make_async_copy(src, cbuf.at[home], c_recv).start()
+                    pltpu.make_async_copy(src, cbuf.at[home], c_recv.at[g]).start()
 
                 @pl.when(q != pc)
                 def _():
-                    remote(src, cbuf.at[home], c_send, c_recv, (pr, q)).start()
+                    remote(src, cbuf.at[home], c_send, c_recv.at[g], (pr, q)).start()
 
             @pl.when(g == 1)
             def _():
@@ -305,98 +311,95 @@
 
         @pl.when(g == 0)
         def _():
-            out_c[:, span(zl * S + c * W, W)] = crow[:, cols]
-
-    def turned(n):
-        return rem(n + y, NCH)
-
-    def second_product():
-        await_bytes(cbuf, c_recv)
-        chi, clo = split(cbuf[...].T)
-
-        @pl.loop(0, NCH)
-        def _(i):
-            n = turned(i)
-            cols = span(n * W, W)
-            dbuf[:, cols] = dot3(chi, clo, xhi[:, cols], xlo[:, cols])
-            d_first(n)
+            for n in range(W // 128):
+                place = pl.ds((c * (W // 128) + n) * NSUP + zl, 32, stride=NSUP * S // 128)
+                out_c[place, :] = crow[:, span(j * W + n * 128, 128)]
+
+    owner_x = 2 * core + rem(y + zh, 2)
+    owner = owner_x * 2 + zh
+
+    def tile_y(target):
+        return rem(y + 6 - owner_x + target, 4)
+
+    def second_product(g):
+        block = span((zl if g == 0 else other) * PART, PART)
+        await_bytes(cbuf.at[block], c_recv.at[g])
+        chi, clo = split(cbuf[block, :].T)
+        for d in (2, 1, 3, 0):
+            target = rem(x + d, NX)
+            for b in range(2):
+                cols = span(b * (S // 2) + tile_y(target) * 256, 256)
+                value = dot3(chi, clo, xhi[block, cols], xlo[block, cols])
+                for u in range(NCH):
+                    part = span(target * 32, 32), pl.ds(u * W + b * 256, 256)
+                    if g == 0:
+                        dbuf[part] = value[u * 32 : u * 32 + 32]
+                    else:
+                        dbuf[part] += value[u * 32 : u * 32 + 32]
+            if g == 1 and d == 2:
+                for u in range(NCH):
+                    d_first(u)
 
     def second_ring():
         @pl.loop(0, NCH)
         def _(n):
-            d_second(turned(n))
-
-    @pl.loop(0, 14)
+            d_second(n)
+
+    def pass_on(n, onward):
+        for half in range(2):
+            relay(chunk(n), half, onward)
+
+    take(chunk(0))
+    first_product(0)
+    pass_on(2, True)
+    y_second(item(0)[2])
+    pass_on(1, False)
+    take(chunk(2))
+    first_product(1)
+    take(chunk(1))
+    first_product(2)
+    y_second(item(1)[2])
+    finish_c(0)
+    await_bytes(abuf.at[1], n_recv)
+    split_rows(1)
+    first_product(3)
+    y_second(item(2)[2])
+    pass_on(3, False)
+
+    @pl.loop(4, ITEMS + LAG2)
     def _(i):
-        @pl.when(jnp.logical_or(i < 3, i == 5))
+        @pl.when(i == 5)
         def _():
-            take(item(i)[1])
-
-        @pl.when(i == 3)
-        def _():
-            await_bytes(abuf.at[1], n_recv)
-            split_rows(1)
+            take(chunk(3))
 
         @pl.when(i < ITEMS)
         def _():
             first_product(i)
 
-        @pl.when(i == 0)
-        def _():
-            relay(chunk(2), True)
-
-        @pl.when(jnp.logical_or(i == 1, i == 3))
-        def _():
-            relay(chunk(i), False)
-
-        @pl.when(jnp.logical_and(i >= LAG1, i < ITEMS + LAG1))
+        @pl.when(jnp.logical_and(i >= 3 + LAG1, i < ITEMS + LAG1))
         def _():
             y_second(item(i - LAG1)[2])
 
-        @pl.when(jnp.logical_and(i >= LAG2, i < ITEMS + LAG2))
+        @pl.when(i >= 1 + LAG2)
         def _():
             finish_c(i - LAG2)
 
-        @pl.when(jnp.logical_and(i == DIAG, core == 0))
-        def _():
-            second_product()
-
-        @pl.when(jnp.logical_and(i == DIAG + 1, core == 0))
-        def _():
-            second_ring()
-
-    @pl.when(core == 1)
-    def _():
-        second_product()
-        second_ring()
-
-    owner = (2 * core + rem(y + zh, 2)) * 2 + zh
+    second_product(0)
+    second_product(1)
+    second_ring()
 
     @pl.loop(0, NCH)
-    def _(j):
-        n = turned(j)
-        dsum[:, span(n * W, W)] = d_total(n)
-        for i in range(W // T):
-            q = n * (W // T) + i
-            src = dsum.at[:, span(q * T, T)]
-            dst = dfin.at[zl, span(div(y, 2) * 128 + x * 32, 32)]
-            own = jnp.logical_and(owner == pr, q == pc)
-
-            @pl.when(own)
-            def _():
-                pltpu.make_async_copy(src, dst, d_recv).start()
-
-            @pl.when(jnp.logical_not(own))
-            def _():
-                remote(src, dst, d_send, d_recv, (owner, q)).start()
+    def _(u):
+        dsum[:, span(u * W, W)] = d_total(u)
+        for n in range(W // T):
+            q = (n // 2) * 8 + tile_y(x) * 2 + n % 2
+            src = dsum.at[:, span(u * W + n * T, T)]
+            dst = dfin.at[zl, span(div(y, 2) * 128 + u * 32, 32)]
+            remote(src, dst, d_send, d_recv, (owner, q)).start()
 
     await_bytes(cout, o_recv)
-    out_c[:, span(other * S, S)] = cout[...]
-    piv_copy.wait()
-    await_bytes(dfin, d_recv)
-    for k in range(NSUP):
-        out_d[k] = piv[k] - dfin[k].T
-
+    for n in range(S // 128):
+        out_c[pl.ds(n * NSUP + other, 32, stride=NSUP * S // 128), :] = cout[:, pl.ds(n * 128, 128)]
     await_bytes(abuf.at[0, pl.ds(0, 120)], m_send)
     await_bytes(abuf.at[0, pl.ds(0, 96)], a_send)
     await_bytes(abuf.at[0], n_send)
@@ -409,11 +412,23 @@
     await_bytes(cout, o_send)
     await_bytes(dxo, dxo_send)
     await_bytes(dxf, dxf_send)
-    await_bytes(cbuf.at[pl.ds(0, 480)], d_send)
-
-    @pl.when(owner != pr)
-    def _():
-        await_bytes(cbuf.at[pl.ds(0, 32)], d_send)
+    await_bytes(cbuf.at[pl.ds(0, 512)], d_send)
+
+    piv_copy.wait()
+    await_bytes(dfin, d_recv)
+    for k in range(NSUP):
+        out_d[k] = piv[k] - dfin[k].T
+
+
+def place(columns, diagonal, out_c, out_d, sem):
+    copies = [
+        pltpu.make_async_copy(columns, out_c, sem.at[0]),
+        pltpu.make_async_copy(diagonal, out_d, sem.at[1]),
+    ]
+    for copy in copies:
+        copy.start()
+    for copy in copies:
+        copy.wait()
 
 
 def body(ancestor_inverse, lower_panel, pivot_inverse, structure):
@@ -427,7 +442,7 @@
         kernel,
         name="selinv",
         out_shape=(
-            jax.ShapeDtypeStruct((32, width), F32),
+            jax.ShapeDtypeStruct((32 * width // 128, 128), F32),
             jax.ShapeDtypeStruct(pivot_inverse.shape, F32),
         ),
         in_specs=[hbm, hbm, hbm, hbm],
@@ -459,22 +474,22 @@
             dma(()),
             dma((NR,)),
             dma(()),
-            dma((NX,)),
-            dma(()),
-            dma((NX,)),
-            dma(()),
-            dma(()),
-            dma(()),
-            dma((2, NCH)),
-            dma(()),
-            dma(()),
-            dma((2, NCH)),
+            dma((2, NX)),
+            dma(()),
+            dma((2, NX)),
+            dma(()),
+            dma(()),
+            dma(()),
+            dma((2, 2 * NCH)),
+            dma(()),
+            dma(()),
+            dma((2, 2 * NCH)),
             dma(()),
             dma((2, ITEMS)),
             dma(()),
             dma((2, ITEMS)),
             dma(()),
-            dma(()),
+            dma((2,)),
             dma(()),
             dma(()),
             dma(()),
@@ -493,6 +508,19 @@
             for v in (ancestor_inverse, panel, pivot_inverse, structure)
         )
     )
+    columns, diagonal = pl.pallas_call(
+        place,
+        name="place",
+        out_shape=(
+            jax.ShapeDtypeStruct(columns.shape, F32),
+            jax.ShapeDtypeStruct(diagonal.shape, F32),
+        ),
+        in_specs=[vmem, vmem],
+        out_specs=(hbm, hbm),
+        scratch_shapes=[dma((2,))],
+        compiler_params=pltpu.CompilerParams(vmem_limit_bytes=2**20),
+    )(columns, diagonal)
+    columns = columns.reshape(32, S // 128, NSUP, 128).transpose(0, 2, 1, 3)
     return columns.reshape(32, NSUP, S), diagonal
 
 

time: 75.3 us -> 74.4 us (0.988)
  local copies, waits for them, and re-layouts: 1.93 us -> 0 us
  Pallas kernels: 72.6 us -> 73.4 us
    reshape x1 -> x0, local copies, waits for them, and re-layouts: 1.23 us -> none  [body(): return (columns.reshape(32, NSUP, S), diagonal)]
    pallas_call x0 -> x1, Pallas kernels: none -> 0.89 us  [body(): pl.pallas_call(place, name='place', out_shape=(jax.ShapeDtypeStruct(colum...]
where the time goes in v6:
time: 74.4 us; the launch traced here: 74 us
  Pallas kernels  73.4 us (99%)
    pallas_call x1, Pallas kernels, body(): pl.pallas_call(kernel, name='selinv', out_shape=(jax.ShapeDtypeStruct((32...  72.5 us

profile of v6, /device:TPU:1, one launch (start us, length us, event | category | flops | bytes accessed | tf_op | source)
XLA Modules:
  0.0 74.0 jit_solution(5785760188832192241)
XLA Ops:
  0.6 72.5 %selinv.1 = (f32[1024,128]{1,0:T(8,128)S(1)}, f32[2,128,256]{2,1,0:T(8,128)S(1)}) custom-call(f32[512,256]{1,0:T(8,128)} %a_hbm.1, f32[16384,128]{1,0:T(8,128)} %bitcast.10, f32[2,128,256]{2,1,0:T(8,128)} %piv_hbm.1, s32[2,64]{1,0:T(2,128)} %structure_hbm.1), custom_call_target="tpu_custom_call" | custom-call | tf_op jit(solution)/shard_map/selinv/pallas_call | solution.py:441
  73.2 0.9 %place.1 = (f32[1024,128]{1,0:T(8,128)}, f32[2,128,256]{2,1,0:T(8,128)}) custom-call(f32[1024,128]{1,0:T(8,128)S(1)} %get-tuple-element.6.columns, f32[2,128,256]{2,1,0:T(8,128)S(1)} %get-tuple-element.7.diagonal), custom_call_target="tpu_custom_call" | custom-call | tf_op jit(solution)/shard_map/place/pallas_call | solution.py:511

commit v7 on v6

--- a/solution.py
+++ b/solution.py
@@ -21,7 +21,6 @@
 NCH = S // W
 ITEMS = 2 * NCH
 EARLY = 5
-LAG1, LAG2 = 2, 4
 H = W // 2
 T = S // NC
 
@@ -77,15 +76,6 @@
     def span(start, size):
         return pl.ds(pl.multiple_of(start, size), size)
 
-    rows = BLK * NSUP * S // 128
-    structure_copy = pltpu.make_async_copy(structure_hbm, structure, structure_sem)
-    structure_copy.start()
-    for i in range(NR):
-        block = pl.ds(i * rows, rows)
-        pltpu.make_async_copy(l_hbm.at[block], lst.at[block], l_sem.at[i]).start()
-    piv_copy = pltpu.make_async_copy(piv_hbm, piv, piv_sem)
-    piv_copy.start()
-
     barrier = pltpu.get_barrier_semaphore()
 
     def greet(device):
@@ -97,6 +87,18 @@
         greet(at_xz(rem(x + j, NX), z))
     greet(z_down)
     greet(z_up)
+    rows = BLK * NSUP * S // 128
+    blocks = [part * 4 + 2 * c + b for c in (core, 1 - core) for part in range(2) for b in range(2)]
+    l_copies = [
+        pltpu.make_async_copy(l_hbm.at[span(i * rows, rows)], lst.at[span(i * rows, rows)], l_sem.at[n])
+        for n, i in enumerate(blocks)
+    ]
+    structure_copy = pltpu.make_async_copy(structure_hbm, structure, structure_sem)
+    structure_copy.start()
+    for copy in l_copies:
+        copy.start()
+    piv_copy = pltpu.make_async_copy(piv_hbm, piv, piv_sem)
+    piv_copy.start()
     pl.semaphore_wait(barrier, NC - 1 + NX - 1 + 2)
 
     def a_piece(q, h):
@@ -113,9 +115,8 @@
             remote(src, dst, m_send, recv, (pr, q)).start()
 
     structure_copy.wait()
-    for i in range(NR):
-        block = pl.ds(i * rows, rows)
-        pltpu.make_async_copy(l_hbm.at[block], lst.at[block], l_sem.at[i]).wait()
+    for copy in l_copies[:4]:
+        copy.wait()
 
     def pack(j):
         for part in range(2):
@@ -208,6 +209,9 @@
         pack(chunk(n))
         send_x(chunk(n))
 
+    for copy in l_copies[4:]:
+        copy.wait()
+
     @pl.loop(0, EARLY)
     def _(i):
         prepare(i)
@@ -270,10 +274,9 @@
     d_first, d_second, d_total = x_stage(dbuf, dxo, dxf, dxo_send, dxo_recv, dxf_send, dxf_recv)
 
     def item(i):
-        own = jnp.logical_or(i < 3, i == 5)
-        g = jnp.where(own, 0, 1)
-        n = jnp.where(i < 3, rem(2 * i, 3), jnp.where(i < 5, i - 3, jnp.where(i == 5, 3, i - 4)))
-        c = chunk(n)
+        own = i < 3 or i == 5
+        n = (2 * i) % 3 if i < 3 else i - 3 if i < 5 else 3 if i == 5 else i - 4
+        g, c = (0 if own else 1), chunk(n)
         return g, c, g * NCH + c
 
     def first_product(i):
@@ -287,8 +290,7 @@
         cols = span(j * W, W)
         value = y_total(j)
         for h, neighbour in enumerate((z_down, z_up)):
-            owner_row = jnp.where(g == 0, pr, neighbour[0])
-            owner_col = jnp.where(g == 0, pc, neighbour[1])
+            owner_row, owner_col = (pr, pc) if g == 0 else neighbour
             mask = structure[zl, owner_row * NR + div(owner_col, 2)].astype(F32)
             part = pl.ds(h * 16, 16)
             crow[part, cols] = -mask * value[h * 16 : h * 16 + 16]
@@ -305,12 +307,10 @@
                 def _():
                     remote(src, cbuf.at[home], c_send, c_recv.at[g], (pr, q)).start()
 
-            @pl.when(g == 1)
-            def _():
+            if g == 1:
                 remote(crow.at[part, cols], cout.at[part, span(c * W, W)], o_send, o_recv, neighbour).start()
 
-        @pl.when(g == 0)
-        def _():
+        if g == 0:
             for n in range(W // 128):
                 place = pl.ds((c * (W // 128) + n) * NSUP + zl, 32, stride=NSUP * S // 128)
                 out_c[place, :] = crow[:, span(j * W + n * 128, 128)]
@@ -366,24 +366,23 @@
     y_second(item(2)[2])
     pass_on(3, False)
 
-    @pl.loop(4, ITEMS + LAG2)
-    def _(i):
-        @pl.when(i == 5)
-        def _():
-            take(chunk(3))
-
-        @pl.when(i < ITEMS)
-        def _():
-            first_product(i)
-
-        @pl.when(jnp.logical_and(i >= 3 + LAG1, i < ITEMS + LAG1))
-        def _():
-            y_second(item(i - LAG1)[2])
-
-        @pl.when(i >= 1 + LAG2)
-        def _():
-            finish_c(i - LAG2)
-
+    first_product(4)
+    take(chunk(3))
+    first_product(5)
+    y_second(item(3)[2])
+    first_product(6)
+    first_product(7)
+    y_second(item(4)[2])
+    y_second(item(5)[2])
+    finish_c(1)
+    finish_c(2)
+    y_second(item(6)[2])
+    finish_c(3)
+    y_second(item(7)[2])
+    finish_c(4)
+    finish_c(5)
+    finish_c(6)
+    finish_c(7)
     second_product(0)
     second_product(1)
     second_ring()

time: 74.4 us -> 73.7 us (level)
    pallas_call x1, Pallas kernels: 72.5 us -> 71.8 us  [body(): pl.pallas_call(kernel, name='selinv', out_shape=(jax.ShapeDtypeStruct((32...]
where the time goes in v7:
time: 73.7 us; the launch traced here: 73.3 us
  Pallas kernels  72.7 us (99%)
    pallas_call x1, Pallas kernels, body(): pl.pallas_call(kernel, name='selinv', out_shape=(jax.ShapeDtypeStruct((32...  71.8 us

profile of v7, /device:TPU:1, one launch (start us, length us, event | category | flops | bytes accessed | tf_op | source)
XLA Modules:
  0.0 73.3 jit_solution(9695385538015496145)
XLA Ops:
  0.6 71.8 %selinv.1 = (f32[1024,128]{1,0:T(8,128)S(1)}, f32[2,128,256]{2,1,0:T(8,128)S(1)}) custom-call(f32[512,256]{1,0:T(8,128)} %a_hbm.1, f32[16384,128]{1,0:T(8,128)} %bitcast.10, f32[2,128,256]{2,1,0:T(8,128)} %piv_hbm.1, s32[2,64]{1,0:T(2,128)} %structure_hbm.1), custom_call_target="tpu_custom_call" | custom-call | tf_op jit(solution)/shard_map/selinv/pallas_call | solution.py:440
  72.4 0.9 %place.1 = (f32[1024,128]{1,0:T(8,128)}, f32[2,128,256]{2,1,0:T(8,128)}) custom-call(f32[1024,128]{1,0:T(8,128)S(1)} %get-tuple-element.6.columns, f32[2,128,256]{2,1,0:T(8,128)S(1)} %get-tuple-element.7.diagonal), custom_call_target="tpu_custom_call" | custom-call | tf_op jit(solution)/shard_map/place/pallas_call | solution.py:510

commit v8 on v7

--- a/solution.py
+++ b/solution.py
@@ -223,10 +223,10 @@
         prepare(i)
 
     forward(1)
+    relay(chunk(0), 0, True)
     share(0)
-    relay(chunk(0), 0, True)
+    relay(chunk(0), 1, True)
     share(1)
-    relay(chunk(0), 1, True)
     split_rows(0)
 
     def x_stage(buf, far, final, far_send, far_recv, final_send, final_recv):
@@ -275,7 +275,7 @@
 
     def item(i):
         own = i < 3 or i == 5
-        n = (2 * i) % 3 if i < 3 else i - 3 if i < 5 else 3 if i == 5 else i - 4
+        n = i if i < 3 else i - 3 if i < 5 else 3 if i == 5 else i - 4
         g, c = (0 if own else 1), chunk(n)
         return g, c, g * NCH + c
 
@@ -345,26 +345,25 @@
         def _(n):
             d_second(n)
 
-    def pass_on(n, onward):
-        for half in range(2):
-            relay(chunk(n), half, onward)
-
     take(chunk(0))
     first_product(0)
-    pass_on(2, True)
+    relay(chunk(2), 0, True)
+    relay(chunk(1), 0, False)
+    relay(chunk(1), 1, False)
     y_second(item(0)[2])
-    pass_on(1, False)
+    relay(chunk(2), 1, True)
+    take(chunk(1))
+    first_product(1)
     take(chunk(2))
-    first_product(1)
-    take(chunk(1))
     first_product(2)
     y_second(item(1)[2])
     finish_c(0)
+    for half in range(2):
+        relay(chunk(3), half, False)
     await_bytes(abuf.at[1], n_recv)
     split_rows(1)
     first_product(3)
     y_second(item(2)[2])
-    pass_on(3, False)
 
     first_product(4)
     take(chunk(3))

time: 73.7 us -> 71.8 us (0.974)
  Pallas kernels: 72.7 us -> 70.8 us
    pallas_call x1, Pallas kernels: 71.8 us -> 69.9 us  [body(): pl.pallas_call(kernel, name='selinv', out_shape=(jax.ShapeDtypeStruct((32...]
where the time goes in v8:
time: 71.8 us; the launch traced here: 71.5 us
  Pallas kernels  70.8 us (99%)
    pallas_call x1, Pallas kernels, body(): pl.pallas_call(kernel, name='selinv', out_shape=(jax.ShapeDtypeStruct((32...  69.9 us

profile of v8, /device:TPU:1, one launch (start us, length us, event | category | flops | bytes accessed | tf_op | source)
XLA Modules:
  0.0 71.5 jit_solution(958028655748897560)
XLA Ops:
  0.6 69.9 %selinv.1 = (f32[1024,128]{1,0:T(8,128)S(1)}, f32[2,128,256]{2,1,0:T(8,128)S(1)}) custom-call(f32[512,256]{1,0:T(8,128)} %a_hbm.1, f32[16384,128]{1,0:T(8,128)} %bitcast.10, f32[2,128,256]{2,1,0:T(8,128)} %piv_hbm.1, s32[2,64]{1,0:T(2,128)} %structure_hbm.1), custom_call_target="tpu_custom_call" | custom-call | tf_op jit(solution)/shard_map/selinv/pallas_call | solution.py:439
  70.6 0.9 %place.1 = (f32[1024,128]{1,0:T(8,128)}, f32[2,128,256]{2,1,0:T(8,128)}) custom-call(f32[1024,128]{1,0:T(8,128)S(1)} %get-tuple-element.6.columns, f32[2,128,256]{2,1,0:T(8,128)S(1)} %get-tuple-element.7.diagonal), custom_call_target="tpu_custom_call" | custom-call | tf_op jit(solution)/shard_map/place/pallas_call | solution.py:509

commit v9 on v8

--- a/solution.py
+++ b/solution.py
@@ -295,9 +295,16 @@
             part = pl.ds(h * 16, 16)
             crow[part, cols] = -mask * value[h * 16 : h * 16 + 16]
             home = span(rem(owner_row, 2) * PART + owner_col * 32 + h * 16, 16)
+            if g == 0 and h == 0:
+                continue
+            if g == 0:
+                sent = pl.ds(0, 32)
+                home = span(zl * PART + pc * 32, 32)
+            else:
+                sent = part
             for n in range(W // T):
                 q = (n // 2) * 8 + ((n % 2) * 2 + rem(c + n // 2, 2)) * 2 + div(c, 2)
-                src = crow.at[part, span(j * W + n * T, T)]
+                src = crow.at[sent, span(j * W + n * T, T)]
 
                 @pl.when(q == pc)
                 def _():
@@ -368,8 +375,8 @@
     first_product(4)
     take(chunk(3))
     first_product(5)
+    first_product(6)
     y_second(item(3)[2])
-    first_product(6)
     first_product(7)
     y_second(item(4)[2])
     y_second(item(5)[2])

time: 71.8 us -> 71.8 us (level)
  no operation moved by 1% of the time
where the time goes in v9:
time: 71.8 us; the launch traced here: 71.5 us
  Pallas kernels  70.8 us (99%)
    pallas_call x1, Pallas kernels, body(): pl.pallas_call(kernel, name='selinv', out_shape=(jax.ShapeDtypeStruct((32...  69.9 us

profile of v9, /device:TPU:1, one launch (start us, length us, event | category | flops | bytes accessed | tf_op | source)
XLA Modules:
  0.0 71.5 jit_solution(15147176920250929318)
XLA Ops:
  0.6 69.9 %selinv.1 = (f32[1024,128]{1,0:T(8,128)S(1)}, f32[2,128,256]{2,1,0:T(8,128)S(1)}) custom-call(f32[512,256]{1,0:T(8,128)} %a_hbm.1, f32[16384,128]{1,0:T(8,128)} %bitcast.10, f32[2,128,256]{2,1,0:T(8,128)} %piv_hbm.1, s32[2,64]{1,0:T(2,128)} %structure_hbm.1), custom_call_target="tpu_custom_call" | custom-call | tf_op jit(solution)/shard_map/selinv/pallas_call | solution.py:446
  70.6 0.9 %place.1 = (f32[1024,128]{1,0:T(8,128)}, f32[2,128,256]{2,1,0:T(8,128)}) custom-call(f32[1024,128]{1,0:T(8,128)S(1)} %get-tuple-element.6.columns, f32[2,128,256]{2,1,0:T(8,128)S(1)} %get-tuple-element.7.diagonal), custom_call_target="tpu_custom_call" | custom-call | tf_op jit(solution)/shard_map/place/pallas_call | solution.py:516
